TPU v7x, 512 devices: a whole 4x8x8 slice. The times are simulated.
512 devices in a mesh: dp: 128 (over z, y, core), mp: 4 (over x).
Axes of the slice: x: 4, y: 8, z: 8, core: 2. Of those that a mesh axis runs over, the one named last changes fastest.
Arguments:
- hot_ids: int32 [131072, 7], P('dp'), may hold values from 0 to 1023
- touched: int32 [128, 4, 256], P('dp', 'mp'), may hold values from 0 to 131071, as said below
- cold_items: int32 [128, 4, 2048], P('dp', 'mp'), may hold values from 0 to 255
- bag_counts: int32 [128, 4, 1024], P('dp', 'mp'), may hold values from 1 to 8, 2048 in all within a row
- owner_map: int32 [131072], replicated, may hold values from 0 to 131071, as said below
- grad_out: bfloat16 [131072, 256], P('dp'), may hold values from -6 to 6
- weight_in: bfloat16 [1024, 512], P(None, 'mp'), may hold values from -0.1875 to 0.1875
- bias_in: float32 [512], P('mp'), may hold values from -4 to 4
- weight_out: bfloat16 [512, 256], P('mp'), may hold values from -0.25 to 0.25
- hot_table: float32 [1024, 128], replicated, may hold values from -6 to 6
- hot_accum: float32 [1024, 128], replicated, may hold values from 0.25 to 4
- cold_table: float32 [131072, 128], P(('dp', 'mp')), may hold values from -6 to 6
- cold_accum: float32 [131072, 128], P(('dp', 'mp')), may hold values from 0.25 to 4
Outputs:
- hot_updated: float32 [1024, 128], replicated
- hot_accum_new: float32 [1024, 128], replicated
- cold_updated: float32 [131072, 128], P(('dp', 'mp'))
- cold_accum_new: float32 [131072, 128], P(('dp', 'mp'))
Inputs may be any that keep to these rules, and one draw needn't show every extreme that they name: owner_map is a permutation of the cold row ids: cold row g is stored in row owner_map[g] of cold_table. `touched`: the 256 ids of one device are distinct, and owner_map sends all of them to rows stored on devices with the same mp index as that device; at most 4 of them are stored on any one dp index, and exactly 4 on some.
All inputs are finite; a program needn't handle non-finite values.
Results may differ from a plain program's by a relative error of at most 0.0038.
Values may be sent and summed in bfloat16 or wider, within the bound.
A program may use at most 64 MiB of HBM per device.

v0:
```python
import jax
import jax.numpy as jnp
from jax import lax
from jax.sharding import PartitionSpec as P

STEP_SIZE = 0.5
HIGHEST = lax.Precision.HIGHEST


def adagrad(table_rows, accum_rows, grad_rows):
    accum_new = accum_rows + grad_rows * grad_rows
    return (table_rows - STEP_SIZE * grad_rows / jnp.sqrt(accum_new), accum_new)


def silu_grad(pre_act, back_grad):
    sigmoid_val = jax.nn.sigmoid(pre_act)
    return (back_grad * sigmoid_val * (1.0 + pre_act * (1.0 - sigmoid_val))).astype(jnp.bfloat16)


def per_device(
    hot_ids,
    touched,
    cold_items,
    bag_counts,
    owner_map,
    grad_out,
    weight_in,
    bias_in,
    weight_out,
    hot_table,
    hot_accum,
    cold_table,
    cold_accum,
):
    dp_count = lax.axis_size("dp")
    mp_count = lax.axis_size("mp")
    slot_count = cold_table.shape[0]
    emb_width = cold_table.shape[1]
    samples = hot_ids.shape[0]
    fields = hot_ids.shape[1]
    hot_cols = fields * emb_width
    touch_count = touched.shape[2]
    capacity = 2 * touch_count // dp_count
    share_rows = samples // mp_count
    my_start = lax.axis_index("mp") * share_rows
    my_ids = touched[0, 0]
    stored_at = owner_map[my_ids]
    owner_dp = stored_at // (mp_count * slot_count)
    slot_index = stored_at % slot_count
    owner_hits = (owner_dp[:, None] == jnp.arange(dp_count, dtype=jnp.int32)[None, :]).astype(
        jnp.float32
    )
    touch_iota = jnp.arange(touch_count, dtype=jnp.int32)
    earlier = (touch_iota[:, None] > touch_iota[None, :]).astype(jnp.float32)
    before_mine = jnp.dot(earlier, owner_hits, precision=HIGHEST)
    rank_owner = jnp.sum(before_mine * owner_hits, axis=1).astype(jnp.int32)
    bucket_pos = owner_dp * capacity + rank_owner
    requests = (
        jnp.zeros((dp_count * capacity,), jnp.int32)
        .at[bucket_pos]
        .set(slot_index)
        .reshape(dp_count, capacity)
    )
    asked_slots = lax.all_to_all(requests, "dp", split_axis=0, concat_axis=0, tiled=True)
    rows_out = cold_table[asked_slots]
    rows_back = lax.all_to_all(rows_out, "dp", split_axis=0, concat_axis=0, tiled=True)
    fetched = rows_back.reshape(dp_count * capacity, emb_width)[bucket_pos]
    bag_sizes = bag_counts[0, 0]
    end_pos = jnp.cumsum(bag_sizes)
    start_pos = end_pos - bag_sizes
    items_here = cold_items[0, 0]
    item_pos = jnp.arange(items_here.shape[0], dtype=jnp.int32)
    member = (
        (item_pos[None, :] >= start_pos[:, None]) & (item_pos[None, :] < end_pos[:, None])
    ).astype(jnp.bfloat16)
    picks = (items_here[:, None] == touch_iota[None, :]).astype(jnp.bfloat16)
    count_mat = jnp.dot(member, picks, preferred_element_type=jnp.float32)
    pooled_part = jnp.dot(count_mat, fetched, precision=HIGHEST)
    my_hot_ids = lax.dynamic_slice_in_dim(hot_ids, my_start, share_rows, 0)
    full_in = lax.all_gather(weight_in, "mp", axis=1, tiled=True)
    full_out = lax.all_gather(weight_out, "mp", axis=0, tiled=True)
    full_bias = lax.all_gather(bias_in, "mp", axis=0, tiled=True)
    pooled_mine = lax.psum_scatter(pooled_part, "mp", scatter_dimension=0, tiled=True)
    my_grads = lax.dynamic_slice_in_dim(grad_out, my_start, share_rows, 0)
    hot_rows = hot_table[my_hot_ids].reshape(share_rows, hot_cols)
    inputs = jnp.concatenate([hot_rows, pooled_mine], axis=1).astype(jnp.bfloat16)
    pre_act = jnp.dot(inputs, full_in, preferred_element_type=jnp.float32) + full_bias
    back_grad = lax.dot_general(
        my_grads, full_out, (((1,), (1,)), ((), ())), preferred_element_type=jnp.float32
    )
    hidden_grad = silu_grad(pre_act, back_grad)
    input_grad = lax.dot_general(
        hidden_grad, full_in, (((1,), (1,)), ((), ())), preferred_element_type=jnp.float32
    )
    hot_part = jax.ops.segment_sum(
        input_grad[:, :hot_cols].reshape(share_rows * fields, emb_width),
        my_hot_ids.reshape(share_rows * fields),
        num_segments=hot_table.shape[0],
    )
    bag_grad = lax.all_gather(input_grad[:, hot_cols:], "mp", axis=0, tiled=True)
    touch_grad = lax.dot_general(count_mat, bag_grad, (((0,), (0,)), ((), ())), precision=HIGHEST)
    outgoing = (
        jnp.zeros((dp_count * capacity, emb_width), jnp.float32)
        .at[bucket_pos]
        .set(touch_grad)
        .reshape(dp_count, capacity, emb_width)
    )
    arrived = lax.all_to_all(outgoing, "dp", split_axis=0, concat_axis=0, tiled=True)
    cold_grad = jax.ops.segment_sum(
        arrived.reshape(-1, emb_width), asked_slots.reshape(-1), num_segments=slot_count
    )
    cold_updated, cold_accum_new = adagrad(cold_table, cold_accum, cold_grad)
    hot_grad = lax.psum(hot_part, ("dp", "mp"))
    hot_updated, hot_accum_new = adagrad(hot_table, hot_accum, hot_grad)
    return (hot_updated, hot_accum_new, cold_updated, cold_accum_new)


def solution(mesh):
    return jax.shard_map(
        per_device,
        mesh=mesh,
        in_specs=(
            P("dp", None),
            P("dp", "mp", None),
            P("dp", "mp", None),
            P("dp", "mp", None),
            P(),
            P("dp", None),
            P(None, "mp"),
            P("mp"),
            P("mp", None),
            P(),
            P(),
            P(("dp", "mp"), None),
            P(("dp", "mp"), None),
        ),
        out_specs=(P(), P(), P(("dp", "mp"), None), P(("dp", "mp"), None)),
        check_vma=False,
    )
```

profile of v0, /device:TPU:1, one launch (start us, length us, event | category | flops | bytes accessed | tf_op | source)
XLA Modules:
  0.0 427.5 jit_solution(7015179249153434986)
XLA Ops:
  8.0 3.5 gather_fusion.1
  11.7 1.4 scatter_custom_fusion
  13.9 18.4 %all-to-all-start = ((s32[128,1,4]{2,1,0:T(1,128)}), s32[128,1,4]{2,1,0:T(1,128)S(1)}, u32[]{:S(2)}, u32[]{:S(2)}) async-start(s32[128,1,4]{2,1,0:T(1,128)} %bitcast.9), calls=%async_computation | async-start | bytes 131072 | tf_op jit(solution)/shard_map/all_to_all | solution.py:64
  32.8 10.9 %all-to-all-done = s32[128,1,4]{2,1,0:T(1,128)S(1)} async-done(((s32[128,1,4]{2,1,0:T(1,128)}), s32[128,1,4]{2,1,0:T(1,128)S(1)}, u32[]{:S(2)}, u32[]{:S(2)}) %all-to-all-start) | async-done | bytes 2080 | tf_op jit(solution)/shard_map/all_to_all | solution.py:64
  43.8 1.6 gather_fusion.2
  45.5 5.8 %all-to-all-start.1 = ((f32[128,4,128]{2,1,0:T(4,128)}), f32[128,4,128]{2,1,0:T(4,128)S(1)}, u32[]{:S(2)}, u32[]{:S(2)}) async-start(f32[128,4,128]{2,1,0:T(4,128)} %bitcast.11), calls=%async_computation.1 | async-start | bytes 524288 | tf_op jit(solution)/shard_map/all_to_all | solution.py:66
  51.4 2.6 fusion.1
  54.0 12.6 %all-to-all-done.1 = f32[128,4,128]{2,1,0:T(4,128)S(1)} async-done(((f32[128,4,128]{2,1,0:T(4,128)}), f32[128,4,128]{2,1,0:T(4,128)S(1)}, u32[]{:S(2)}, u32[]{:S(2)}) %all-to-all-start.1) | async-done | bytes 262176 | tf_op jit(solution)/shard_map/all_to_all | solution.py:66
  67.3 1.8 fusion.37
  71.4 3.2 gather_fusion
  75.1 8.0 %all-gather = f32[4,1,128]{2,1,0:T(1,128)S(1)} all-gather(f32[1,1,128]{2,1,0:T(1,128)S(1)} %bitcast.43), channel_id=1, replica_groups=mesh['dp'=128,'mp'=4] {'mp'}, dimensions={0}, use_global_device_ids=true | all-gather | bytes 2560 | tf_op jit(solution)/shard_map/all_gather | solution.py:82
  83.1 10.3 %all_gather.12 = bf16[512,256]{1,0:T(8,128)(2,1)} all-gather(bf16[128,256]{1,0:T(8,128)(2,1)S(1)} %copy-done.6), channel_id=1, replica_groups=mesh['dp'=128,'mp'=4] {'mp'}, dimensions={0}, use_global_device_ids=true | all-gather | bytes 327680 | tf_op jit(solution)/shard_map/all_gather | solution.py:81
  94.3 26.3 %all-gather.3.cloned.1.call-done = bf16[1024,512]{1,0:T(8,128)(2,1)} async-done(((bf16[1024,128]{1,0:T(8,128)(2,1)}), bf16[1024,512]{1,0:T(8,128)(2,1)}) %all-gather.3.cloned.1.call-update) | async-done | bytes 1048592 | tf_op jit(solution)/shard_map/all_gather | solution.py:80
  120.6 2.5 convolution_add_fusion
  123.1 2.1 fusion.7
  126.2 1.2 slice.26
  128.5 12.6 %scatter_custom_fusion.1 = f32[1024,128]{1,0:T(8,128)} fusion(s32[1792]{0:T(1024)S(1)} %reshape.248, f32[1792,128]{1,0:T(8,128)} %reshape.250, f32[]{:T(128)} %constant.20.clone.1), kind=kCustom, calls=%fused_computation.37 | custom fusion | flops 229376 | bytes 524800 | tf_op jit(solution)/shard_map/scatter-add | solution.py:95
  141.1 11.3 %all_gather.15 = f32[1024,128]{1,0:T(8,128)S(1)} all-gather(f32[256,128]{1,0:T(8,128)S(1)} %slice-done), channel_id=1, replica_groups=mesh['dp'=128,'mp'=4] {'mp'}, dimensions={0}, use_global_device_ids=true | all-gather | bytes 655360 | tf_op jit(solution)/shard_map/all_gather | solution.py:100
  152.4 1.8 fusion.38
  154.2 1.8 scatter_custom_fusion.2
  156.1 17.4 %all-to-all-start.2 = ((f32[128,4,128]{2,1,0:T(4,128)}), f32[128,4,128]{2,1,0:T(4,128)S(1)}, u32[]{:S(2)}, u32[]{:S(2)}) async-start(f32[128,4,128]{2,1,0:T(4,128)} %bitcast.15), calls=%async_computation.3 | async-start | bytes 524288 | tf_op jit(solution)/shard_map/all_to_all | solution.py:108
  174.9 240.9 %all-reduce.2.cloned.1.call-done = f32[1024,128]{1,0:T(8,128)} async-done(((f32[1024,128]{1,0:T(8,128)}), f32[1024,128]{1,0:T(8,128)}) %all-reduce.2.cloned.1.call-update) | async-done | bytes 524304 | tf_op jit(solution)/shard_map/psum | solution.py:113
  415.8 2.1 multiply_subtract_fusion
  417.9 2.3 scatter_custom_fusion.3
  (60 shorter events, 11.0 us)
Async XLA Ops:
  7.2 115.9 %copy-start = (bf16[1024,256]{1,0:T(8,128)(2,1)S(1)}, bf16[1024,256]{1,0:T(8,128)(2,1)}, u32[]{:S(2)}) copy-start(bf16[1024,256]{1,0:T(8,128)(2,1)} %param.18) | copy-start | bytes 1572868
  7.2 25.1 %copy-start.7 = (s32[1,1,1024]{2,1,0:T(1,128)S(1)}, s32[1,1,1024]{2,1,0:T(1,128)}, u32[]{:S(2)}) copy-start(s32[1,1,1024]{2,1,0:T(1,128)} %param.16) | copy-start | bytes 12292
  7.2 36.6 %copy-start.2 = (f32[256,128]{1,0:T(8,128)S(1)}, f32[256,128]{1,0:T(8,128)}, u32[]{:S(2)}) copy-start(f32[256,128]{1,0:T(8,128)} %param.24) | copy-start | bytes 393220
  13.9 29.8 %all-to-all-start = ((s32[128,1,4]{2,1,0:T(1,128)}), s32[128,1,4]{2,1,0:T(1,128)S(1)}, u32[]{:S(2)}, u32[]{:S(2)}) async-start(s32[128,1,4]{2,1,0:T(1,128)} %bitcast.9), calls=%async_computation | async-start | bytes 131072 | tf_op jit(solution)/shard_map/all_to_all | solution.py:64
  43.8 7.6 %copy-start.9 = (s32[1,1,2048]{2,1,0:T(1,128)S(1)}, s32[1,1,2048]{2,1,0:T(1,128)}, u32[]{:S(2)}) copy-start(s32[1,1,2048]{2,1,0:T(1,128)} %param.15) | copy-start | bytes 24580
  45.5 21.1 %all-to-all-start.1 = ((f32[128,4,128]{2,1,0:T(4,128)}), f32[128,4,128]{2,1,0:T(4,128)S(1)}, u32[]{:S(2)}, u32[]{:S(2)}) async-start(f32[128,4,128]{2,1,0:T(4,128)} %bitcast.11), calls=%async_computation.1 | async-start | bytes 524288 | tf_op jit(solution)/shard_map/all_to_all | solution.py:66
  51.2 42.2 %reduce-scatter.2.cloned.1.call-start = ((), (), s32[]{:S(2)}) async-start(), calls=%async_computation.4 | async-start | bytes 655360 | tf_op jit(solution)/shard_map/reduce_scatter | solution.py:83
  69.1 2.3 copy-start.1
  69.1 51.5 %all-gather.3.cloned.1.call-start = ((), (), s32[]{:S(2)}) async-start(), calls=%async_computation.5 | async-start | bytes 1310720 | tf_op jit(solution)/shard_map/all_gather | solution.py:80
  69.9 345.9 %all-reduce.2.cloned.1.call-start = ((), (), s32[]{:S(2)}) async-start(), calls=%async_computation.6 | async-start | bytes 1048576 | tf_op jit(solution)/shard_map/psum | solution.py:113
  71.4 3.7 copy-start.8
  71.4 11.7 %copy-start.6 = (bf16[128,256]{1,0:T(8,128)(2,1)S(1)}, bf16[128,256]{1,0:T(8,128)(2,1)}, u32[]{:S(2)}) copy-start(bf16[128,256]{1,0:T(8,128)(2,1)} %param.21) | copy-start | bytes 196612
  125.2 1.0 copy-start.3
  127.4 13.7 %slice-start = ((f32[256,1024]{1,0:T(8,128)}), f32[256,128]{1,0:T(8,128)S(1)}, s32[]{:S(2)}) async-start(f32[256,1024]{1,0:T(8,128)} %copy-done.3), calls=%async_computation.7 | async-start | bytes 262144 | tf_op jit(solution)/shard_map/slice | solution.py:100
  152.4 263.4 %copy-start.4 = (f32[1024,128]{1,0:T(8,128)S(1)}, f32[1024,128]{1,0:T(8,128)}, u32[]{:S(2)}) copy-start(f32[1024,128]{1,0:T(8,128)} %param.23) | copy-start | bytes 1572868
  156.1 261.9 %all-to-all-start.2 = ((f32[128,4,128]{2,1,0:T(4,128)}), f32[128,4,128]{2,1,0:T(4,128)S(1)}, u32[]{:S(2)}, u32[]{:S(2)}) async-start(f32[128,4,128]{2,1,0:T(4,128)} %bitcast.15), calls=%async_computation.3 | async-start | bytes 524288 | tf_op jit(solution)/shard_map/all_to_all | solution.py:108
  174.9 245.4 %copy-start.5 = (f32[256,128]{1,0:T(8,128)S(1)}, f32[256,128]{1,0:T(8,128)}, u32[]{:S(2)}) copy-start(f32[256,128]{1,0:T(8,128)} %param.25) | copy-start | bytes 393220
Sparse Core Ops, SparseCore 0:
  69.3 17.2 reduce-scatter.1
  88.6 31.9 all-gather.2
  141.2 274.5 all-reduce.1
where the time goes:
time: 428 us; the launch traced here: 427 us
  waiting for transfers between devices  291 us (68%)
  starting transfers between devices  41.7 us (10%)
  blocking collectives  29.6 us (7%)
  other arithmetic  21.4 us (5%)
  local copies, waits for them, and re-layouts  18.3 us (4%)
  between operations  14 us (3%)
  matrix products  11 us (3%)
    psum x1, waiting for transfers between devices, per_device(): hot_grad = lax.psum(hot_part, ('dp', 'mp'))  241 us
    all_gather x1, waiting for transfers between devices, per_device(): full_in = lax.all_gather(weight_in, 'mp', axis=1, tiled=True)  26.3 us
    all_to_all x1, starting transfers between devices, per_device(): lax.all_to_all(requests, 'dp', split_axis=0, concat_axis=0, tiled=True)  18.4 us
    all_to_all x1, starting transfers between devices, per_device(): lax.all_to_all(outgoing, 'dp', split_axis=0, concat_axis=0, tiled=True)  17.4 us
    scatter-add x1, other arithmetic, per_device(): jax.ops.segment_sum(input_grad[:, :hot_cols].reshape(share_rows * fields,...  12.6 us
    all_to_all x1, waiting for transfers between devices, per_device(): lax.all_to_all(rows_out, 'dp', split_axis=0, concat_axis=0, tiled=True)  12.6 us
    all_gather x1, blocking collectives, per_device(): lax.all_gather(input_grad[:, hot_cols:], 'mp', axis=0, tiled=True)  11.3 us
    all_to_all x1, waiting for transfers between devices, per_device(): lax.all_to_all(requests, 'dp', split_axis=0, concat_axis=0, tiled=True)  10.9 us
  transfers between devices with their start and end apart: 6, of which 4 were waited for; matrix products, arithmetic and copies ran while one was open for 4% of the time, Pallas kernels for 0%

commit v1 on v0

--- a/solution.py
+++ b/solution.py
@@ -1,10 +1,141 @@
+import functools
+
 import jax
 import jax.numpy as jnp
 from jax import lax
+from jax.experimental import pallas as pl
+from jax.experimental.pallas import tpu as pltpu
 from jax.sharding import PartitionSpec as P
 
 STEP_SIZE = 0.5
 HIGHEST = lax.Precision.HIGHEST
+
+MESH = pl.DeviceIdType.MESH
+NY, NZ = 8, 8
+
+def coords():
+    dp, mp = lax.axis_index("dp"), lax.axis_index("mp")
+    return dp // 16, (dp // 2) % 8, dp % 2, mp
+
+def dev(z, y, c, x):
+    return (z * 16 + y * 2 + c, x)
+
+def hot_allreduce_kernel(part, full, r_core, a_half, r_x, a_x, r_z, b_y, snd, rcv):
+    z, y, c, x = coords()
+    barrier = pltpu.get_barrier_semaphore()
+    peers = [dev(z, y, 1 - c, x)]
+    peers += [dev(z, y, c, (x + o) % 4) for o in range(1, 4)]
+    peers += [dev((z + o) % 8, y, c, x) for o in range(1, 8)]
+    peers += [dev(z, (y + o) % 8, c, x) for o in range(1, 8)]
+    for p in peers:
+        pl.semaphore_signal(barrier, inc=1, device_id=p, device_id_type=MESH)
+    pl.semaphore_wait(barrier, len(peers))
+    n = [0]
+    def copy(src, dst, to):
+        k = n[0]; n[0] += 1
+        cp = pltpu.make_async_remote_copy(src_ref=src, dst_ref=dst, send_sem=snd.at[k], recv_sem=rcv.at[k],
+                                          device_id=to, device_id_type=MESH)
+        cp.start()
+        return cp
+    sends = []
+    other = pl.multiple_of((1 - c) * 512, 512)
+    mine = pl.multiple_of(c * 512, 512)
+    cp = copy(part.at[pl.ds(other, 512)], r_core, dev(z, y, 1 - c, x))
+    cp.wait_recv(); sends.append(cp)
+    a_half[...] = part[pl.ds(mine, 512)] + r_core[...]
+    cps = []
+    for o in range(1, 4):
+        xo = (x + o) % 4
+        cps.append(copy(a_half.at[pl.ds(pl.multiple_of(xo * 128, 128), 128)], r_x.at[o - 1], dev(z, y, c, xo)))
+    for cp in cps: cp.wait_recv()
+    sends += cps
+    a_x[...] = a_half[pl.ds(pl.multiple_of(x * 128, 128), 128)] + r_x[0] + r_x[1] + r_x[2]
+    cps = []
+    for o in range(1, 8):
+        zo = (z + o) % 8
+        cps.append(copy(a_x.at[pl.ds(pl.multiple_of(zo * 16, 16), 16)], r_z.at[o - 1], dev(zo, y, c, x)))
+    for cp in cps: cp.wait_recv()
+    sends += cps
+    s = a_x[pl.ds(pl.multiple_of(z * 16, 16), 16)]
+    for o in range(7): s += r_z[o]
+    b_y[y] = s
+    cps = []
+    for o in range(1, 8):
+        yo = (y + o) % 8
+        cps.append(copy(b_y.at[y], b_y.at[y], dev(z, yo, c, x)))
+    for cp in cps: cp.wait_recv()
+    sends += cps
+    s = b_y[0]
+    for o in range(1, 8): s += b_y[o]
+    own = pl.ds(pl.multiple_of(c * 512 + x * 128 + z * 16, 16), 16)
+    full[own] = s
+    cps = []
+    for o in range(1, 8):
+        cps.append(copy(full.at[own], full.at[own], dev((z + o) % 8, y, c, x)))
+    for cp in cps: cp.wait_recv()
+    sends += cps
+    own = pl.ds(pl.multiple_of(c * 512 + x * 128, 128), 128)
+    cps = []
+    for o in range(1, 4):
+        cps.append(copy(full.at[own], full.at[own], dev(z, y, c, (x + o) % 4)))
+    sends += cps
+    fw = [copy(full.at[own], full.at[own], dev(z, y, 1 - c, x))]
+    for o, cp in zip(range(1, 4), cps):
+        cp.wait_recv()
+        blk = pl.ds(pl.multiple_of(c * 512 + ((x + 4 - o) % 4) * 128, 128), 128)
+        fw.append(copy(full.at[blk], full.at[blk], dev(z, y, 1 - c, x)))
+    for cp in fw: cp.wait_recv()
+    sends += fw
+    for cp in sends: cp.wait_send()
+
+def hot_allreduce(part, cid=0):
+    f = jnp.float32
+    ncp = 1 + 3 + 7 + 7 + 7 + 3 + 4
+    return pl.pallas_call(
+        hot_allreduce_kernel,
+        out_shape=jax.ShapeDtypeStruct((1024, 128), f),
+        in_specs=[pl.BlockSpec(memory_space=pltpu.VMEM)],
+        out_specs=pl.BlockSpec(memory_space=pltpu.VMEM),
+        scratch_shapes=[pltpu.VMEM((512, 128), f), pltpu.VMEM((512, 128), f), pltpu.VMEM((3, 128, 128), f),
+                        pltpu.VMEM((128, 128), f), pltpu.VMEM((7, 16, 128), f), pltpu.VMEM((8, 16, 128), f),
+                        pltpu.SemaphoreType.DMA((ncp,)), pltpu.SemaphoreType.DMA((ncp,))],
+        compiler_params=pltpu.CompilerParams(collective_id=cid, has_side_effects=True, vmem_limit_bytes=32 << 20),
+    )(part)
+
+
+def exchange_kernel(x_ref, o_ref, snd, rcv):
+    dp, mp = lax.axis_index("dp"), lax.axis_index("mp")
+    barrier = pltpu.get_barrier_semaphore()
+
+    @pl.loop(1, 128)
+    def _(o):
+        pl.semaphore_signal(barrier, inc=1, device_id=((dp + o) % 128, mp), device_id_type=MESH)
+
+    pl.semaphore_wait(barrier, 127)
+
+    @pl.loop(1, 128)
+    def _(o):
+        to = (dp + o) % 128
+        pltpu.make_async_remote_copy(
+            src_ref=x_ref.at[to], dst_ref=o_ref.at[dp], send_sem=snd, recv_sem=rcv,
+            device_id=(to, mp), device_id_type=MESH,
+        ).start()
+
+    o_ref[dp] = x_ref[dp]
+    pltpu.make_async_copy(o_ref.at[pl.ds(0, 127)], o_ref.at[pl.ds(0, 127)], rcv).wait()
+    pltpu.make_async_copy(x_ref.at[pl.ds(0, 127)], x_ref.at[pl.ds(0, 127)], snd).wait()
+
+
+def exchange(x, cid):
+    vmem = pl.BlockSpec(memory_space=pltpu.VMEM)
+    return pl.pallas_call(
+        exchange_kernel,
+        out_shape=jax.ShapeDtypeStruct(x.shape, x.dtype),
+        in_specs=[vmem],
+        out_specs=vmem,
+        scratch_shapes=[pltpu.SemaphoreType.DMA, pltpu.SemaphoreType.DMA],
+        compiler_params=pltpu.CompilerParams(collective_id=cid, has_side_effects=True),
+    )(x)
 
 
 def adagrad(table_rows, accum_rows, grad_rows):
@@ -61,12 +192,14 @@
         .set(slot_index)
         .reshape(dp_count, capacity)
     )
-    asked_slots = lax.all_to_all(requests, "dp", split_axis=0, concat_axis=0, tiled=True)
+    padded = jnp.pad(requests, ((0, 0), (0, 124))).reshape(dp_count, 1, 128)
+    asked_slots = exchange(padded, 1)[:, 0, :capacity]
     rows_out = cold_table[asked_slots]
-    rows_back = lax.all_to_all(rows_out, "dp", split_axis=0, concat_axis=0, tiled=True)
+    rows_back = exchange(rows_out, 2)
     fetched = rows_back.reshape(dp_count * capacity, emb_width)[bucket_pos]
     bag_sizes = bag_counts[0, 0]
-    end_pos = jnp.cumsum(bag_sizes)
+    upto = (jnp.arange(samples)[:, None] >= jnp.arange(samples)[None, :]).astype(jnp.bfloat16)
+    end_pos = jnp.dot(upto, bag_sizes.astype(jnp.bfloat16), preferred_element_type=jnp.float32).astype(jnp.int32)
     start_pos = end_pos - bag_sizes
     items_here = cold_items[0, 0]
     item_pos = jnp.arange(items_here.shape[0], dtype=jnp.int32)
@@ -105,12 +238,12 @@
         .set(touch_grad)
         .reshape(dp_count, capacity, emb_width)
     )
-    arrived = lax.all_to_all(outgoing, "dp", split_axis=0, concat_axis=0, tiled=True)
+    arrived = exchange(outgoing, 3)
     cold_grad = jax.ops.segment_sum(
         arrived.reshape(-1, emb_width), asked_slots.reshape(-1), num_segments=slot_count
     )
     cold_updated, cold_accum_new = adagrad(cold_table, cold_accum, cold_grad)
-    hot_grad = lax.psum(hot_part, ("dp", "mp"))
+    hot_grad = hot_allreduce(hot_part, 0)
     hot_updated, hot_accum_new = adagrad(hot_table, hot_accum, hot_grad)
     return (hot_updated, hot_accum_new, cold_updated, cold_accum_new)
 

time: 428 us -> 227 us (0.53)
  waiting for transfers between devices: 291 us -> 30.8 us
  Pallas kernels: 0 us -> 103 us
  starting transfers between devices: 41.7 us -> 0.08 us
    psum x1 -> x0, waiting for transfers between devices: 241 us -> none  [per_device(): hot_grad = lax.psum(hot_part, ('dp', 'mp'))]
    pallas_call x0 -> x4, Pallas kernels: none -> 103 us  [the longest x3 65.1 us: exchange(): pl.pallas_call(exchange_kernel, out_shape=jax.ShapeDtypeStruct(x.shape, x...]
    all_to_all x3 -> x0, starting transfers between devices: 41.6 us -> none  [the longest x1 18.4 us: per_device(): lax.all_to_all(requests, 'dp', split_axis=0, concat_axis=0, tiled=True)]
    all_to_all x3 -> x0, waiting for transfers between devices: 23.5 us -> none  [the longest x1 12.6 us: per_device(): lax.all_to_all(rows_out, 'dp', split_axis=0, concat_axis=0, tiled=True)]
  transfers between devices with their start and end apart: 6 -> 2, of which waited for: 4 -> 1; matrix products, arithmetic and copies ran while one was open for 4% -> 3% of each run, Pallas kernels for 0% -> 0%
where the time goes in v1:
time: 227 us; the launch traced here: 226 us
  Pallas kernels  103 us (45%)
  waiting for transfers between devices  30.8 us (14%)
  blocking collectives  28.8 us (13%)
  other arithmetic  19.4 us (9%)
  local copies, waits for them, and re-layouts  17.9 us (8%)
  between operations  14.4 us (6%)
  matrix products  11.4 us (5%)
    pallas_call x3, Pallas kernels, exchange(): pl.pallas_call(exchange_kernel, out_shape=jax.ShapeDtypeStruct(x.shape, x...  65.1 us
    pallas_call x1, Pallas kernels, hot_allreduce(): pl.pallas_call(hot_allreduce_kernel, out_shape=jax.ShapeDtypeStruct((1024...  38.2 us
    all_gather x1, waiting for transfers between devices, per_device(): full_in = lax.all_gather(weight_in, 'mp', axis=1, tiled=True)  30.1 us
    scatter-add x1, other arithmetic, per_device(): jax.ops.segment_sum(input_grad[:, :hot_cols].reshape(share_rows * fields,...  12.2 us
    all_gather x1, blocking collectives, per_device(): lax.all_gather(input_grad[:, hot_cols:], 'mp', axis=0, tiled=True)  10.8 us
    all_gather x1, blocking collectives, per_device(): full_out = lax.all_gather(weight_out, 'mp', axis=0, tiled=True)  9.93 us
    all_gather x1, blocking collectives, per_device(): full_bias = lax.all_gather(bias_in, 'mp', axis=0, tiled=True)  8 us
  transfers between devices with their start and end apart: 2, of which 1 were waited for; matrix products, arithmetic and copies ran while one was open for 3% of the time, Pallas kernels for 0%

profile of v1, /device:TPU:1, one launch (start us, length us, event | category | flops | bytes accessed | tf_op | source)
XLA Modules:
  0.0 226.0 jit_solution(14013700489420425691)
XLA Ops:
  8.6 1.7 gather_fusion.1
  10.6 1.4 scatter_custom_fusion
  12.8 24.1 %shard_map.156 = s32[128,1,128]{2,1,0:T(1,128)} custom-call(s32[128,1,128]{2,1,0:T(1,128)} %bitcast.34), custom_call_target="tpu_custom_call" | custom-call | tf_op jit(solution)/shard_map/pallas_call | solution.py:131
  38.1 1.6 gather_fusion.2
  39.7 20.6 %shard_map.157 = f32[128,4,128]{2,1,0:T(4,128)} custom-call(f32[128,4,128]{2,1,0:T(4,128)} %bitcast.30), custom_call_target="tpu_custom_call" | custom-call | tf_op jit(solution)/shard_map/pallas_call | solution.py:131
  60.3 1.7 gather_fusion.3
  62.0 2.6 %fusion.1 = f32[1024,256]{1,0:T(8,128)S(1)} fusion(s32[1024]{0:T(1024)S(1)} %convert_element_type.29, s32[1024]{0:T(1024)S(1)} %convert_subtract_fusion, s32[2048]{0:T(1024)S(1)} %bitcast.47), kind=kOutput, calls=%fused_computation.11 | convolution fusion | flops 1080557568 | bytes 1064960 | tf_op jit(solution)/shard_map/dot_general | solution.py:210
  64.6 1.8 fusion.37
  68.7 3.2 %gather_fusion = bf16[1792,128]{1,0:T(8,128)(2,1)S(1)} fusion(f32[1024,128]{1,0:T(8,128)S(1)} %copy-done.1, s32[2048]{0:T(1024)S(1)} %pad_clamp_fusion), kind=kCustom, calls=%fused_computation | custom fusion | bytes 924672 | tf_op jit(solution)/shard_map/gather | solution.py:218
  72.4 8.0 %all-gather = f32[4,1,128]{2,1,0:T(1,128)S(1)} all-gather(f32[1,1,128]{2,1,0:T(1,128)S(1)} %bitcast.46), channel_id=1, replica_groups=mesh['dp'=128,'mp'=4] {'mp'}, dimensions={0}, use_global_device_ids=true | all-gather | bytes 2560 | tf_op jit(solution)/shard_map/all_gather | solution.py:215
  80.4 9.9 %all_gather.12 = bf16[512,256]{1,0:T(8,128)(2,1)S(1)} all-gather(bf16[128,256]{1,0:T(8,128)(2,1)S(1)} %copy-done.7), channel_id=1, replica_groups=mesh['dp'=128,'mp'=4] {'mp'}, dimensions={0}, use_global_device_ids=true | all-gather | bytes 327680 | tf_op jit(solution)/shard_map/all_gather | solution.py:214
  91.3 30.1 %all-gather.3.cloned.1.call-done = bf16[1024,512]{1,0:T(8,128)(2,1)} async-done(((bf16[1024,128]{1,0:T(8,128)(2,1)}), bf16[1024,512]{1,0:T(8,128)(2,1)}) %all-gather.3.cloned.1.call-update) | async-done | bytes 1048592 | tf_op jit(solution)/shard_map/all_gather | solution.py:213
  121.3 2.5 %convolution_add_fusion = f32[256,512]{1,0:T(8,128)} fusion(bf16[1024,512]{1,0:T(8,128)(2,1)} %all-gather.3.cloned.1.call-done, bf16[256,128]{1,0:T(8,128)(2,1)S(1)} %convert.8, bf16[256,896]{1,0:T(8,128)(2,1)S(1)} %reshape.164, f32[512]{0:T(512)S(1)} %bitcast.45), kind=kOutput, calls=%fused_computation.17 | convolution fusion | flops 269615104 | bytes 2099200 | tf_op jit(solution)/shard_map/dot_general | solution.py:220
  123.8 2.0 fusion.8
  126.8 1.2 slice.20
  128.0 1.1 reshape.215
  129.1 12.2 %scatter_custom_fusion.1.part = f32[1024,128]{1,0:T(8,128)S(1)} fusion(s32[1792]{0:T(1024)S(1)} %reshape.213, f32[1792,128]{1,0:T(8,128)} %reshape.215, f32[]{:T(128)} %constant.18.clone.1), kind=kCustom, calls=%fused_computation.39 | custom fusion | flops 229376 | bytes 524800 | tf_op jit(solution)/shard_map/scatter-add | solution.py:228
  141.3 38.2 %shard_map.158 = f32[1024,128]{1,0:T(8,128)S(1)} custom-call(f32[1024,128]{1,0:T(8,128)S(1)} %scatter_custom_fusion.1.part), custom_call_target="tpu_custom_call" | custom-call | tf_op jit(solution)/shard_map/pallas_call | solution.py:94
  179.5 10.8 %all_gather.15 = f32[1024,128]{1,0:T(8,128)S(1)} all-gather(f32[256,128]{1,0:T(8,128)S(1)} %slice-done), channel_id=1, replica_groups=mesh['dp'=128,'mp'=4] {'mp'}, dimensions={0}, use_global_device_ids=true | all-gather | bytes 655360 | tf_op jit(solution)/shard_map/all_gather | solution.py:233
  190.4 1.8 fusion.38
  192.2 1.8 scatter_custom_fusion.2
  194.0 20.4 %shard_map.159 = f32[128,4,128]{2,1,0:T(4,128)} custom-call(f32[128,4,128]{2,1,0:T(4,128)} %bitcast.31), custom_call_target="tpu_custom_call" | custom-call | tf_op jit(solution)/shard_map/pallas_call | solution.py:131
  214.4 2.9 %scatter_custom_fusion.3 = f32[256,128]{1,0:T(8,128)S(1)} fusion(s32[512]{0:T(512)S(1)} %reshape.229, f32[512,128]{1,0:T(8,128)} %bitcast.33, f32[]{:T(128)} %constant.18.clone.1), kind=kCustom, calls=%fused_computation.48 | custom fusion | flops 65536 | bytes 131584 | tf_op jit(solution)/shard_map/scatter-add | solution.py:242
  218.1 1.1 multiply_subtract_fusion
  (59 shorter events, 8.9 us)
Async XLA Ops:
  7.2 116.6 %copy-start = (bf16[1024,256]{1,0:T(8,128)(2,1)S(1)}, bf16[1024,256]{1,0:T(8,128)(2,1)}, u32[]{:S(2)}) copy-start(bf16[1024,256]{1,0:T(8,128)(2,1)} %param.18) | copy-start | bytes 1572868
  7.2 1.3 copy-start.8
  7.2 1.3 copy-start.9
  7.2 1.4 copy-start.3
  7.2 83.1 %reduce-scatter.2.cloned.1.call-start = ((), (), s32[]{:S(2)}) async-start(), calls=%async_computation.1 | async-start | bytes 655360 | tf_op jit(solution)/shard_map/reduce_scatter | solution.py:216
  8.5 29.6 %copy-start.2 = (f32[256,128]{1,0:T(8,128)S(1)}, f32[256,128]{1,0:T(8,128)}, u32[]{:S(2)}) copy-start(f32[256,128]{1,0:T(8,128)} %param.24) | copy-start | bytes 393220
  39.7 22.3 %copy-start.11 = (s32[1,1,2048]{2,1,0:T(1,128)S(1)}, s32[1,1,2048]{2,1,0:T(1,128)}, u32[]{:S(2)}) copy-start(s32[1,1,2048]{2,1,0:T(1,128)} %param.15) | copy-start | bytes 24580
  66.4 2.3 %copy-start.1 = (f32[1024,128]{1,0:T(8,128)S(1)}, f32[1024,128]{1,0:T(8,128)}, u32[]{:S(2)}) copy-start(f32[1024,128]{1,0:T(8,128)} %param.22) | copy-start | bytes 1572868
  66.4 54.9 %all-gather.3.cloned.1.call-start = ((), (), s32[]{:S(2)}) async-start(), calls=%async_computation.2 | async-start | bytes 1310720 | tf_op jit(solution)/shard_map/all_gather | solution.py:213
  68.7 3.7 %copy-start.10 = (f32[128]{0:T(128)S(1)}, f32[128]{0:T(128)}, u32[]{:S(2)}) copy-start(f32[128]{0:T(128)} %param.20) | copy-start | bytes 1540
  68.7 11.7 %copy-start.7 = (bf16[128,256]{1,0:T(8,128)(2,1)S(1)}, bf16[128,256]{1,0:T(8,128)(2,1)}, u32[]{:S(2)}) copy-start(bf16[128,256]{1,0:T(8,128)(2,1)} %param.21) | copy-start | bytes 196612
  125.8 1.0 copy-start.4
  129.1 50.4 %slice-start = ((f32[256,1024]{1,0:T(8,128)}), f32[256,128]{1,0:T(8,128)S(1)}, s32[]{:S(2)}) async-start(f32[256,1024]{1,0:T(8,128)} %copy-done.4), calls=%async_computation.3 | async-start | bytes 262144 | tf_op jit(solution)/shard_map/slice | solution.py:233
  190.4 26.9 %copy-start.6 = (f32[256,128]{1,0:T(8,128)S(1)}, f32[256,128]{1,0:T(8,128)}, u32[]{:S(2)}) copy-start(f32[256,128]{1,0:T(8,128)} %param.25) | copy-start | bytes 393220
  192.2 25.9 %copy-start.5 = (f32[1024,128]{1,0:T(8,128)S(1)}, f32[1024,128]{1,0:T(8,128)}, u32[]{:S(2)}) copy-start(f32[1024,128]{1,0:T(8,128)} %param.23) | copy-start | bytes 1572868
Sparse Core Ops, SparseCore 0:
  66.5 20.3 reduce-scatter.1
  89.0 32.3 all-gather.2

commit v2 on v0

v2 whole, which is shorter than its diff:
```python
import functools

import jax
import jax.numpy as jnp
from jax import lax
from jax.experimental import pallas as pl
from jax.experimental.pallas import tpu as pltpu
from jax.sharding import PartitionSpec as P

STEP_SIZE = 0.5
MESH = pl.DeviceIdType.MESH
F32, BF16, I32 = jnp.float32, jnp.bfloat16, jnp.int32
NT = (((1,), (1,)), ((), ()))


def adagrad(table_rows, accum_rows, grad_rows):
    accum_new = accum_rows + grad_rows * grad_rows
    return (table_rows - STEP_SIZE * grad_rows / jnp.sqrt(accum_new), accum_new)


def iota(shape, dim):
    return lax.broadcasted_iota(I32, shape, dim)


def mm(a, b):
    return jnp.dot(a, b, preferred_element_type=F32)


def mm_nt(a, b):
    return lax.dot_general(a, b, NT, preferred_element_type=F32)


def ones_where(mask):
    return jnp.where(mask, 1.0, 0.0).astype(BF16)


def halves(x):
    high = x.astype(BF16)
    low = (x - high.astype(F32)).astype(BF16)
    return jnp.concatenate([high, low], axis=1)


def joined(x):
    half = x.shape[1] // 2
    return x[:, :half] + x[:, half:]


def column(row):
    parts = [
        jnp.broadcast_to(row[:, k : k + 128], (128, 128)).T for k in range(0, row.shape[1], 128)
    ]
    return parts[0] if len(parts) == 1 else jnp.concatenate(parts, axis=0)


def rows_at(index, size):
    return pl.ds(pl.multiple_of(index * size, size), size)


def step_kernel(
    ids_ref, touched_ref, items_ref, counts_ref, owner_ref, grad_ref, win_ref, bias_ref, wout_ref,
    hot_ref, cold_ref, hot_grad, cold_grad,
    full_in, full_out, full_bias, req, asked, rows_out, rows_back, member, picks, bag_mat, bag_mat_t,
    gather_t, hot_in, hot_pre, back, pooled, pool_in, bag, part, part_in, acc, acc_in, sums, outgoing,
    arrived, sem_w, sem_pool, sem_bag, sem_a, sem_d, sem_x,
):
    dp, x = lax.axis_index("dp"), lax.axis_index("mp")
    core = dp % 2
    plane = dp // 2

    def near(ox):
        return (dp, (x + ox) % 4)

    barrier = pltpu.get_barrier_semaphore()
    for ox in range(1, 4):
        pl.semaphore_signal(barrier, inc=1, device_id=near(ox), device_id_type=MESH)

    @pl.loop(1, 128)
    def _(o):
        pl.semaphore_signal(barrier, inc=1, device_id=((dp + o) % 128, x), device_id_type=MESH)

    touched = column(touched_ref[0].astype(F32)).astype(I32)
    lane = iota((256, 128), 1)
    owner_row = touched >> 7
    picked = jnp.concatenate(
        [ones_where(owner_row == lane + 128 * k) for k in range(8)], axis=1
    )
    owners = owner_ref[...]
    tables = jnp.concatenate(
        [(owners >> 10).astype(F32).astype(BF16), (owners & 255).astype(F32).astype(BF16)], axis=1
    )
    found = mm(picked, tables)
    here = (touched & 127) == lane
    owner = jnp.sum(jnp.where(here, found[:, :128], 0.0), axis=1, keepdims=True)
    slot = jnp.sum(jnp.where(here, found[:, 128:], 0.0), axis=1, keepdims=True)
    lane_f = lane.astype(F32)
    hits = jnp.where(owner == lane_f, 1.0, 0.0)
    earlier = ones_where(iota((256, 256), 0) > iota((256, 256), 1))
    rank = jnp.sum(mm(earlier, hits.astype(BF16)) * hits, axis=1, keepdims=True)
    ranked = jnp.where(rank == lane_f, slot + 1.0, 0.0).astype(BF16)
    req[:, 0, :] = mm(hits.T.astype(BF16), ranked)
    bucket = owner * 4.0 + rank

    pl.semaphore_wait(barrier, 130)

    def send_all(src, dst, k):
        @pl.loop(1, 128)
        def _(o):
            to = (dp + o) % 128
            pltpu.make_async_remote_copy(
                src_ref=src.at[to], dst_ref=dst.at[dp], send_sem=sem_x.at[0, k], recv_sem=sem_x.at[1, k],
                device_id=(to, x), device_id_type=MESH,
            ).start()
        dst[dp] = src[dp]

    def wait_all(src, dst, k):
        some = dst.at[pl.ds(0, 127)]
        pltpu.make_async_copy(some, some, sem_x.at[1, k]).wait()

    def wait_sent(src, k):
        some = src.at[pl.ds(0, 127)]
        pltpu.make_async_copy(some, some, sem_x.at[0, k]).wait()

    def to_near(ox, src, dst, sems, k):
        cp = pltpu.make_async_remote_copy(
            src_ref=src, dst_ref=dst, send_sem=sems.at[0, k], recv_sem=sems.at[1, k],
            device_id=near(ox), device_id_type=MESH,
        )
        cp.start()
        return cp

    send_all(req, asked, 0)

    mine = rows_at(x, 128)
    weight_copies = []
    for ox in range(1, 4):
        weight_copies.append(to_near(ox, win_ref, full_in.at[:, mine], sem_w, ox - 1))
        weight_copies.append(to_near(ox, wout_ref, full_out.at[mine], sem_w, ox + 2))
        weight_copies.append(to_near(ox, bias_ref, full_bias.at[:, mine], sem_w, ox + 5))
    full_in[:, mine] = win_ref[...]
    full_out[mine] = wout_ref[...]
    full_bias[:, mine] = bias_ref[...]

    counts = counts_ref[0].astype(F32)
    eight = jnp.concatenate([counts[:, 128 * j : 128 * (j + 1)] for j in range(8)], axis=0)
    upto = ones_where(iota((128, 128), 0) <= iota((128, 128), 1))
    ends = mm(eight.astype(BF16), upto)
    total = jnp.zeros((1, 1), F32)
    item_pos = iota((128, 2048), 1).astype(F32)
    for j in range(8):
        end = ends[j : j + 1] + total
        total = end[:, 127:128]
        end_col = column(end)[:, :1]
        start_col = column(end - eight[j : j + 1])[:, :1]
        member[128 * j : 128 * (j + 1)] = ones_where((item_pos >= start_col) & (item_pos < end_col))
    picks[...] = ones_where(items_ref[0] == iota((256, 2048), 0))

    wait_all(req, asked, 0)

    wanted = asked[:, 0, :].astype(BF16)
    spread = mm(ones_where((iota((512, 128), 0) >> 2) == iota((512, 128), 1)), wanted)
    wanted_col = jnp.sum(
        jnp.where((iota((512, 128), 0) & 3) == iota((512, 128), 1), spread, 0.0), axis=1, keepdims=True
    )
    chosen = ones_where(wanted_col == (iota((512, 256), 1) + 1).astype(F32))
    rows_out[...] = joined(mm(chosen, halves(cold_ref[...]))).reshape(128, 4, 128)
    send_all(rows_out, rows_back, 1)

    count_mat = mm_nt(member[...], picks[...]).astype(BF16)
    spot = jnp.where(bucket == iota((256, 512), 1).astype(F32), 1.0, 0.0)
    bag_mat[...] = mm(count_mat, spot.astype(BF16)).astype(BF16)
    count_mat_t = mm_nt(picks[...], member[...]).astype(BF16)
    bag_mat_t[...] = mm(spot.T.astype(BF16), count_mat_t).astype(BF16)

    share = rows_at(x, 256)
    ids = ids_ref[:, share]
    hot_bf = hot_ref[...].astype(BF16)
    row_of = iota((1024, 256), 0)
    lane_1k = iota((256, 1024), 1).astype(F32)
    for f in range(7):
        one = ids[f : f + 1]
        gather_t[:, 256 * f : 256 * (f + 1)] = ones_where(row_of == one)
        pick_f = ones_where(column(one.astype(F32))[:, :1] == lane_1k)
        hot_in[:, 128 * f : 128 * (f + 1)] = mm(pick_f, hot_bf).astype(BF16)
    for cp in weight_copies:
        cp.wait_recv()
    hot_pre[...] = mm(hot_in[...], full_in[0:896]) + full_bias[...]
    back[...] = mm_nt(grad_ref[share], full_out[...])

    wait_all(rows_out, rows_back, 1)
    pooled[...] = joined(mm(bag_mat[...], halves(rows_back[...].reshape(512, 128))))
    pool_copies = [
        to_near(ox, pooled.at[rows_at((x + ox) % 4, 256)], pool_in.at[ox - 1], sem_pool, ox - 1)
        for ox in range(1, 4)
    ]
    pool_sum = pooled[share]
    for cp in pool_copies:
        cp.wait_recv()
    pool_sum = pool_sum + pool_in[0] + pool_in[1] + pool_in[2]

    pre = hot_pre[...] + mm(pool_sum.astype(BF16), full_in[896:1024])
    gate = jax.nn.sigmoid(pre)
    hidden = (back[...] * gate * (1.0 + pre * (1.0 - gate))).astype(BF16)
    bag[x] = mm_nt(hidden, full_in[896:1024])
    bag_copies = [to_near(ox, bag.at[x], bag.at[x], sem_bag, ox - 1) for ox in range(1, 4)]
    in_grad = jnp.concatenate(
        [halves(mm_nt(hidden, full_in[128 * f : 128 * (f + 1)])) for f in range(7)], axis=0
    )

    a_copies = []
    for oc, ox in ((1, 2), (0, 2), (1, 1), (1, 3), (0, 1), (0, 3), (1, 0), (0, 0)):
        there = rows_at(((core + oc) % 2) * 4 + (x + ox) % 4, 128)
        part[there] = joined(mm(gather_t[there], in_grad))
        k = oc * 4 + ox
        if k:
            cp = pltpu.make_async_remote_copy(
                src_ref=part.at[there], dst_ref=part_in.at[k - 1], send_sem=sem_a.at[0, k - 1],
                recv_sem=sem_a.at[1, k - 1], device_id=(plane * 2 + (core + oc) % 2, (x + ox) % 4),
                device_id_type=MESH,
            )
            cp.start()
            a_copies.append(cp)
    for cp in a_copies:
        cp.wait_recv()
    block = part[rows_at(core * 4 + x, 128)]
    for k in range(7):
        block = block + part_in[k]
    acc[...] = block.reshape(64, 2, 128)

    @pl.loop(1, 64)
    def _(o):
        to = (plane + o) % 64
        pltpu.make_async_remote_copy(
            src_ref=acc.at[to], dst_ref=acc_in.at[plane], send_sem=sem_x.at[0, 2], recv_sem=sem_x.at[1, 2],
            device_id=(to * 2 + core, x), device_id_type=MESH,
        ).start()

    acc_in[plane] = acc[plane]

    for cp in bag_copies:
        cp.wait_recv()
    bag_all = halves(bag[...].reshape(1024, 128))
    outgoing[...] = joined(mm(bag_mat_t[...], bag_all)).reshape(128, 4, 128)

    pltpu.make_async_copy(acc_in.at[pl.ds(0, 63)], acc_in.at[pl.ds(0, 63)], sem_x.at[1, 2]).wait()
    sums[plane] = jnp.sum(acc_in[...], axis=0)

    @pl.loop(1, 64)
    def _(o):
        to = (plane + o) % 64
        pltpu.make_async_remote_copy(
            src_ref=sums.at[plane], dst_ref=sums.at[plane], send_sem=sem_x.at[0, 3], recv_sem=sem_x.at[1, 3],
            device_id=(to * 2 + core, x), device_id_type=MESH,
        ).start()

    send_all(outgoing, arrived, 4)
    wanted_rows = jnp.broadcast_to(wanted_col, (512, 128)).T[0:1]
    chosen_t = ones_where(wanted_rows == (iota((256, 512), 0) + 1).astype(F32))
    pltpu.make_async_copy(sums.at[pl.ds(0, 63)], sums.at[pl.ds(0, 63)], sem_x.at[1, 3]).wait()

    own = rows_at(core * 4 + x, 128)
    hot_grad[own] = sums[...].reshape(128, 128)
    d_copies = []

    def spread_block(rows, to, k):
        cp = pltpu.make_async_remote_copy(
            src_ref=hot_grad.at[rows], dst_ref=hot_grad.at[rows], send_sem=sem_d.at[0, k],
            recv_sem=sem_d.at[1, k], device_id=to, device_id_type=MESH,
        )
        cp.start()
        return cp

    sibling = (plane * 2 + 1 - core, x)
    d_copies = [spread_block(own, near(ox), ox - 1) for ox in range(1, 4)]
    forwards = [spread_block(own, sibling, 3)]
    for ox in (1, 3, 2):
        d_copies[ox - 1].wait_recv()
        forwards.append(spread_block(rows_at(core * 4 + (x + 4 - ox) % 4, 128), sibling, 3 + ox))

    wait_all(outgoing, arrived, 4)
    cold_grad[...] = joined(mm(chosen_t, halves(arrived[...].reshape(512, 128))))
    for cp in forwards:
        cp.wait_recv()

    for cp in weight_copies + pool_copies + bag_copies + a_copies + d_copies + forwards:
        cp.wait_send()
    wait_sent(req, 0)
    wait_sent(rows_out, 1)
    wait_sent(outgoing, 4)
    pltpu.make_async_copy(acc.at[pl.ds(0, 63)], acc.at[pl.ds(0, 63)], sem_x.at[0, 2]).wait()
    pltpu.make_async_copy(sums.at[pl.ds(0, 63)], sums.at[pl.ds(0, 63)], sem_x.at[0, 3]).wait()


def per_device(
    hot_ids, touched, cold_items, bag_counts, owner_map, grad_out, weight_in, bias_in, weight_out,
    hot_table, hot_accum, cold_table, cold_accum,
):
    vmem = pl.BlockSpec(memory_space=pltpu.VMEM)
    v = pltpu.VMEM
    dma = pltpu.SemaphoreType.DMA
    hot_grad, cold_grad = pl.pallas_call(
        step_kernel,
        out_shape=(jax.ShapeDtypeStruct((1024, 128), F32), jax.ShapeDtypeStruct((256, 128), F32)),
        in_specs=[vmem] * 11,
        out_specs=(vmem, vmem),
        scratch_shapes=[
            v((1024, 512), BF16), v((512, 256), BF16), v((1, 512), F32),
            v((128, 1, 128), F32), v((128, 1, 128), F32),
            v((128, 4, 128), F32), v((128, 4, 128), F32),
            v((1024, 2048), BF16), v((256, 2048), BF16), v((1024, 512), BF16), v((512, 1024), BF16),
            v((1024, 1792), BF16), v((256, 896), BF16), v((256, 512), F32), v((256, 512), F32),
            v((1024, 128), F32), v((3, 256, 128), F32), v((4, 256, 128), F32),
            v((1024, 128), F32), v((7, 128, 128), F32), v((64, 2, 128), F32), v((64, 2, 128), F32),
            v((64, 2, 128), F32),
            v((128, 4, 128), F32), v((128, 4, 128), F32),
            dma((2, 9)), dma((2, 3)), dma((2, 3)), dma((2, 7)), dma((2, 7)), dma((2, 5)),
        ],
        compiler_params=pltpu.CompilerParams(
            collective_id=0, has_side_effects=True, vmem_limit_bytes=56 << 20
        ),
        name="step",
    )(
        hot_ids.T, touched, cold_items, bag_counts, owner_map.reshape(1024, 128), grad_out, weight_in,
        bias_in.reshape(1, 128), weight_out, hot_table, cold_table,
    )
    cold_updated, cold_accum_new = adagrad(cold_table, cold_accum, cold_grad)
    hot_updated, hot_accum_new = adagrad(hot_table, hot_accum, hot_grad)
    return (hot_updated, hot_accum_new, cold_updated, cold_accum_new)


def solution(mesh):
    return jax.shard_map(
        per_device,
        mesh=mesh,
        in_specs=(
            P("dp", None),
            P("dp", "mp", None),
            P("dp", "mp", None),
            P("dp", "mp", None),
            P(),
            P("dp", None),
            P(None, "mp"),
            P("mp"),
            P("mp", None),
            P(),
            P(),
            P(("dp", "mp"), None),
            P(("dp", "mp"), None),
        ),
        out_specs=(P(), P(), P(("dp", "mp"), None), P(("dp", "mp"), None)),
        check_vma=False,
    )
```

time: 428 us -> 88.7 us (0.21)
  waiting for transfers between devices: 291 us -> 0 us
  Pallas kernels: 0 us -> 84.9 us
  starting transfers between devices: 41.7 us -> 0 us
  blocking collectives: 29.6 us -> 0 us
  other arithmetic: 21.4 us -> 2.88 us
  local copies, waits for them, and re-layouts: 18.3 us -> 0.03 us
  between operations: 14 us -> 0.7 us
  matrix products: 11 us -> 0 us
    psum x1 -> x0, waiting for transfers between devices: 241 us -> none  [per_device(): hot_grad = lax.psum(hot_part, ('dp', 'mp'))]
    pallas_call x0 -> x1, Pallas kernels: none -> 84.9 us  [per_device(): pl.pallas_call(step_kernel, out_shape=(jax.ShapeDtypeStruct((1024, 128),...]
    all_to_all x3 -> x0, starting transfers between devices: 41.6 us -> none  [the longest x1 18.4 us: per_device(): lax.all_to_all(requests, 'dp', split_axis=0, concat_axis=0, tiled=True)]
    all_gather x3 -> x0, blocking collectives: 29.6 us -> none  [the longest x1 11.3 us: per_device(): lax.all_gather(input_grad[:, hot_cols:], 'mp', axis=0, tiled=True)]
    all_gather x1 -> x0, waiting for transfers between devices: 26.3 us -> none  [per_device(): full_in = lax.all_gather(weight_in, 'mp', axis=1, tiled=True)]
    all_to_all x3 -> x0, waiting for transfers between devices: 23.5 us -> none  [the longest x1 12.6 us: per_device(): lax.all_to_all(rows_out, 'dp', split_axis=0, concat_axis=0, tiled=True)]
    scatter-add x2 -> x0, other arithmetic: 14.9 us -> none  [the longest x1 12.6 us: per_device(): jax.ops.segment_sum(input_grad[:, :hot_cols].reshape(share_rows * fields,...]
    dot_general x6 -> x0, matrix products: 11 us -> none  [the longest x1 2.62 us: per_device(): count_mat = jnp.dot(member, picks, preferred_element_type=jnp.float32)]
  transfers between devices with their start and end apart: 6 -> 0, of which waited for: 4 -> 0; matrix products, arithmetic and copies ran while one was open for 4% -> 0% of each run, Pallas kernels for 0% -> 0%
where the time goes in v2:
time: 88.7 us; the launch traced here: 88.5 us
  Pallas kernels  84.9 us (96%)
  other arithmetic  2.88 us (3%)
    pallas_call x1, Pallas kernels, per_device(): pl.pallas_call(step_kernel, out_shape=(jax.ShapeDtypeStruct((1024, 128),...  84.9 us
    sub x2, other arithmetic, adagrad(): return (table_rows - STEP_SIZE * grad_rows / jnp.sqrt(accum_new), accum_new)  2.88 us

profile of v2, /device:TPU:1, one launch (start us, length us, event | category | flops | bytes accessed | tf_op | source)
XLA Modules:
  0.0 88.5 jit_solution(13925364482328788439)
XLA Ops:
  0.6 0.0 copy-start
  0.6 0.0 copy-start.1
  0.7 84.9 %step.1 = (f32[1024,128]{1,0:T(8,128)}, f32[256,128]{1,0:T(8,128)}) custom-call(s32[7,1024]{1,0:T(8,128)} %bitcast.4, s32[1,1,256]{2,1,0:T(1,128)} %touched_ref.1, s32[1,1,2048]{2,1,0:T(1,128)} %items_ref.1, s32[1,1,1024]{2,1,0:T(1,128)} %counts_ref.1, s32[1024,128]{1,0:T(8,128)} %bitcast.3, bf16[1024,256]{1,0:T(8,128)(2,1)} %grad_ref.1, ...), custom_call_target="tpu_custom_call" | custom-call | tf_op jit(solution)/shard_map/step/pallas_call | solution.py:300
  85.6 0.0 copy-done
  85.6 0.0 copy-done.1
  85.6 0.0 copy-start.2
  85.6 0.0 copy-start.3
  85.6 0.0 copy-start.4
  85.6 2.2 %multiply_subtract_fusion = (f32[1024,128]{1,0:T(8,128)}, f32[1024,128]{1,0:T(8,128)}) fusion(f32[1024,128]{1,0:T(8,128)S(1)} %copy-done, f32[1024,128]{1,0:T(8,128)} %get-tuple-element.6, f32[1024,128]{1,0:T(8,128)S(1)} %copy-done.1), kind=kLoop, calls=%fused_computation | loop fusion | flops 655360 | bytes 2621440 | tf_op jit(solution)/shard_map/sub | solution.py:18
  87.8 0.0 copy-done.2
  87.8 0.0 copy-done.3
  87.8 0.0 copy-done.4
  87.8 0.7 multiply_subtract_fusion.1
Async XLA Ops:
  0.6 84.9 %copy-start = (f32[1024,128]{1,0:T(8,128)S(1)}, f32[1024,128]{1,0:T(8,128)}, u32[]{:S(2)}) copy-start(f32[1024,128]{1,0:T(8,128)} %hot_ref.1) | copy-start | bytes 1572868
  0.6 84.9 %copy-start.1 = (f32[1024,128]{1,0:T(8,128)S(1)}, f32[1024,128]{1,0:T(8,128)}, u32[]{:S(2)}) copy-start(f32[1024,128]{1,0:T(8,128)} %param.23) | copy-start | bytes 1572868
  85.6 2.2 %copy-start.2 = (f32[256,128]{1,0:T(8,128)S(1)}, f32[256,128]{1,0:T(8,128)}, u32[]{:S(2)}) copy-start(f32[256,128]{1,0:T(8,128)} %cold_ref.1) | copy-start | bytes 393220
  85.6 2.2 %copy-start.3 = (f32[256,128]{1,0:T(8,128)S(1)}, f32[256,128]{1,0:T(8,128)}, u32[]{:S(2)}) copy-start(f32[256,128]{1,0:T(8,128)} %param.25) | copy-start | bytes 393220
  85.6 2.2 %copy-start.4 = (f32[256,128]{1,0:T(8,128)S(1)}, f32[256,128]{1,0:T(8,128)}, u32[]{:S(2)}) copy-start(f32[256,128]{1,0:T(8,128)} %get-tuple-element.7) | copy-start | bytes 393220

commit v3 on v2

--- a/solution.py
+++ b/solution.py
@@ -13,9 +13,15 @@
 NT = (((1,), (1,)), ((), ()))
 
 
-def adagrad(table_rows, accum_rows, grad_rows):
-    accum_new = accum_rows + grad_rows * grad_rows
-    return (table_rows - STEP_SIZE * grad_rows / jnp.sqrt(accum_new), accum_new)
+def adagrad_kernel(hot_grad, cold_grad, hot, hot_acc, cold, cold_acc, hot_new, hot_acc_new, cold_new, cold_acc_new):
+    for grad, table, accum, table_new, accum_new in (
+        (hot_grad, hot, hot_acc, hot_new, hot_acc_new),
+        (cold_grad, cold, cold_acc, cold_new, cold_acc_new),
+    ):
+        g = grad[...]
+        a = accum[...] + g * g
+        accum_new[...] = a
+        table_new[...] = table[...] - STEP_SIZE * g * lax.rsqrt(a)
 
 
 def iota(shape, dim):
@@ -61,7 +67,7 @@
     hot_ref, cold_ref, hot_grad, cold_grad,
     full_in, full_out, full_bias, req, asked, rows_out, rows_back, member, picks, bag_mat, bag_mat_t,
     gather_t, hot_in, hot_pre, back, pooled, pool_in, bag, part, part_in, acc, acc_in, sums, outgoing,
-    arrived, sem_w, sem_pool, sem_bag, sem_a, sem_d, sem_x,
+    arrived, hot_own, cold_own, grad_own, sem_l, sem_w, sem_pool, sem_bag, sem_a, sem_d, sem_x,
 ):
     dp, x = lax.axis_index("dp"), lax.axis_index("mp")
     core = dp % 2
@@ -74,9 +80,20 @@
     for ox in range(1, 4):
         pl.semaphore_signal(barrier, inc=1, device_id=near(ox), device_id_type=MESH)
 
-    @pl.loop(1, 128)
-    def _(o):
+    for o in range(1, 128):
         pl.semaphore_signal(barrier, inc=1, device_id=((dp + o) % 128, x), device_id_type=MESH)
+
+    share = rows_at(x, 256)
+    mine = rows_at(x, 128)
+    local = [
+        pltpu.make_async_copy(src, dst, sem_l.at[k])
+        for k, (src, dst) in enumerate((
+            (cold_ref, cold_own), (win_ref, full_in.at[:, mine]), (wout_ref, full_out.at[mine]),
+            (bias_ref, full_bias.at[:, mine]), (hot_ref, hot_own), (grad_ref.at[share], grad_own),
+        ))
+    ]
+    for cp in local:
+        cp.start()
 
     touched = column(touched_ref[0].astype(F32)).astype(I32)
     lane = iota((256, 128), 1)
@@ -130,15 +147,11 @@
 
     send_all(req, asked, 0)
 
-    mine = rows_at(x, 128)
     weight_copies = []
     for ox in range(1, 4):
         weight_copies.append(to_near(ox, win_ref, full_in.at[:, mine], sem_w, ox - 1))
         weight_copies.append(to_near(ox, wout_ref, full_out.at[mine], sem_w, ox + 2))
         weight_copies.append(to_near(ox, bias_ref, full_bias.at[:, mine], sem_w, ox + 5))
-    full_in[:, mine] = win_ref[...]
-    full_out[mine] = wout_ref[...]
-    full_bias[:, mine] = bias_ref[...]
 
     counts = counts_ref[0].astype(F32)
     eight = jnp.concatenate([counts[:, 128 * j : 128 * (j + 1)] for j in range(8)], axis=0)
@@ -153,6 +166,8 @@
         start_col = column(end - eight[j : j + 1])[:, :1]
         member[128 * j : 128 * (j + 1)] = ones_where((item_pos >= start_col) & (item_pos < end_col))
     picks[...] = ones_where(items_ref[0] == iota((256, 2048), 0))
+    local[0].wait()
+    cold_halves = halves(cold_own[...])
 
     wait_all(req, asked, 0)
 
@@ -162,7 +177,7 @@
         jnp.where((iota((512, 128), 0) & 3) == iota((512, 128), 1), spread, 0.0), axis=1, keepdims=True
     )
     chosen = ones_where(wanted_col == (iota((512, 256), 1) + 1).astype(F32))
-    rows_out[...] = joined(mm(chosen, halves(cold_ref[...]))).reshape(128, 4, 128)
+    rows_out[...] = joined(mm(chosen, cold_halves)).reshape(128, 4, 128)
     send_all(rows_out, rows_back, 1)
 
     count_mat = mm_nt(member[...], picks[...]).astype(BF16)
@@ -171,9 +186,10 @@
     count_mat_t = mm_nt(picks[...], member[...]).astype(BF16)
     bag_mat_t[...] = mm(spot.T.astype(BF16), count_mat_t).astype(BF16)
 
-    share = rows_at(x, 256)
+    for cp in local[1:]:
+        cp.wait()
     ids = ids_ref[:, share]
-    hot_bf = hot_ref[...].astype(BF16)
+    hot_bf = hot_own[...].astype(BF16)
     row_of = iota((1024, 256), 0)
     lane_1k = iota((256, 1024), 1).astype(F32)
     for f in range(7):
@@ -184,24 +200,25 @@
     for cp in weight_copies:
         cp.wait_recv()
     hot_pre[...] = mm(hot_in[...], full_in[0:896]) + full_bias[...]
-    back[...] = mm_nt(grad_ref[share], full_out[...])
+    back[...] = mm_nt(grad_own[...], full_out[...])
 
     wait_all(rows_out, rows_back, 1)
-    pooled[...] = joined(mm(bag_mat[...], halves(rows_back[...].reshape(512, 128))))
-    pool_copies = [
-        to_near(ox, pooled.at[rows_at((x + ox) % 4, 256)], pool_in.at[ox - 1], sem_pool, ox - 1)
-        for ox in range(1, 4)
-    ]
-    pool_sum = pooled[share]
+    rows = halves(rows_back[...].reshape(512, 128))
+    pool_copies = []
+    for ox in (2, 1, 3):
+        there = rows_at((x + ox) % 4, 256)
+        pooled[there] = joined(mm(bag_mat[there], rows)).astype(BF16)
+        pool_copies.append(to_near(ox, pooled.at[there], pool_in.at[ox - 1], sem_pool, ox - 1))
+    pool_sum = joined(mm(bag_mat[share], rows))
     for cp in pool_copies:
         cp.wait_recv()
-    pool_sum = pool_sum + pool_in[0] + pool_in[1] + pool_in[2]
+    for k in range(3):
+        pool_sum = pool_sum + pool_in[k].astype(F32)
 
     pre = hot_pre[...] + mm(pool_sum.astype(BF16), full_in[896:1024])
     gate = jax.nn.sigmoid(pre)
     hidden = (back[...] * gate * (1.0 + pre * (1.0 - gate))).astype(BF16)
     bag[x] = mm_nt(hidden, full_in[896:1024])
-    bag_copies = [to_near(ox, bag.at[x], bag.at[x], sem_bag, ox - 1) for ox in range(1, 4)]
     in_grad = jnp.concatenate(
         [halves(mm_nt(hidden, full_in[128 * f : 128 * (f + 1)])) for f in range(7)], axis=0
     )
@@ -219,6 +236,7 @@
             )
             cp.start()
             a_copies.append(cp)
+    bag_copies = [to_near(ox, bag.at[x], bag.at[x], sem_bag, ox - 1) for ox in (2, 1, 3)]
     for cp in a_copies:
         cp.wait_recv()
     block = part[rows_at(core * 4 + x, 128)]
@@ -236,11 +254,6 @@
 
     acc_in[plane] = acc[plane]
 
-    for cp in bag_copies:
-        cp.wait_recv()
-    bag_all = halves(bag[...].reshape(1024, 128))
-    outgoing[...] = joined(mm(bag_mat_t[...], bag_all)).reshape(128, 4, 128)
-
     pltpu.make_async_copy(acc_in.at[pl.ds(0, 63)], acc_in.at[pl.ds(0, 63)], sem_x.at[1, 2]).wait()
     sums[plane] = jnp.sum(acc_in[...], axis=0)
 
@@ -252,6 +265,11 @@
             device_id=(to * 2 + core, x), device_id_type=MESH,
         ).start()
 
+    for cp in bag_copies:
+        cp.wait_recv()
+    bag_all = halves(bag[...].reshape(1024, 128))
+    outgoing[...] = joined(mm(bag_mat_t[...], bag_all)).reshape(128, 4, 128)
+
     send_all(outgoing, arrived, 4)
     wanted_rows = jnp.broadcast_to(wanted_col, (512, 128)).T[0:1]
     chosen_t = ones_where(wanted_rows == (iota((256, 512), 0) + 1).astype(F32))
@@ -259,7 +277,6 @@
 
     own = rows_at(core * 4 + x, 128)
     hot_grad[own] = sums[...].reshape(128, 128)
-    d_copies = []
 
     def spread_block(rows, to, k):
         cp = pltpu.make_async_remote_copy(
@@ -270,7 +287,7 @@
         return cp
 
     sibling = (plane * 2 + 1 - core, x)
-    d_copies = [spread_block(own, near(ox), ox - 1) for ox in range(1, 4)]
+    d_copies = [spread_block(own, near(ox), ox - 1) for ox in (1, 2, 3)]
     forwards = [spread_block(own, sibling, 3)]
     for ox in (1, 3, 2):
         d_copies[ox - 1].wait_recv()
@@ -299,8 +316,8 @@
     dma = pltpu.SemaphoreType.DMA
     hot_grad, cold_grad = pl.pallas_call(
         step_kernel,
-        out_shape=(jax.ShapeDtypeStruct((1024, 128), F32), jax.ShapeDtypeStruct((256, 128), F32)),
-        in_specs=[vmem] * 11,
+        out_shape=(v((1024, 128), F32), v((256, 128), F32)),
+        in_specs=[vmem] * 5 + [pl.BlockSpec(memory_space=pl.ANY)] * 6,
         out_specs=(vmem, vmem),
         scratch_shapes=[
             v((1024, 512), BF16), v((512, 256), BF16), v((1, 512), F32),
@@ -308,10 +325,11 @@
             v((128, 4, 128), F32), v((128, 4, 128), F32),
             v((1024, 2048), BF16), v((256, 2048), BF16), v((1024, 512), BF16), v((512, 1024), BF16),
             v((1024, 1792), BF16), v((256, 896), BF16), v((256, 512), F32), v((256, 512), F32),
-            v((1024, 128), F32), v((3, 256, 128), F32), v((4, 256, 128), F32),
+            v((1024, 128), BF16), v((3, 256, 128), BF16), v((4, 256, 128), F32),
             v((1024, 128), F32), v((7, 128, 128), F32), v((64, 2, 128), F32), v((64, 2, 128), F32),
             v((64, 2, 128), F32),
             v((128, 4, 128), F32), v((128, 4, 128), F32),
+            v((1024, 128), F32), v((256, 128), F32), v((256, 256), BF16), dma((6,)),
             dma((2, 9)), dma((2, 3)), dma((2, 3)), dma((2, 7)), dma((2, 7)), dma((2, 5)),
         ],
         compiler_params=pltpu.CompilerParams(
@@ -322,9 +340,14 @@
         hot_ids.T, touched, cold_items, bag_counts, owner_map.reshape(1024, 128), grad_out, weight_in,
         bias_in.reshape(1, 128), weight_out, hot_table, cold_table,
     )
-    cold_updated, cold_accum_new = adagrad(cold_table, cold_accum, cold_grad)
-    hot_updated, hot_accum_new = adagrad(hot_table, hot_accum, hot_grad)
-    return (hot_updated, hot_accum_new, cold_updated, cold_accum_new)
+    return pl.pallas_call(
+        adagrad_kernel,
+        out_shape=tuple(jax.ShapeDtypeStruct(r.shape, F32) for r in (hot_table, hot_accum, cold_table, cold_accum)),
+        in_specs=[vmem] * 6,
+        out_specs=(vmem,) * 4,
+        compiler_params=pltpu.CompilerParams(vmem_limit_bytes=16 << 20),
+        name="adagrad",
+    )(hot_grad, cold_grad, hot_table, hot_accum, cold_table, cold_accum)
 
 
 def solution(mesh):

time: 88.7 us -> 78 us (0.88)
  Pallas kernels: 84.9 us -> 77.1 us
  other arithmetic: 2.88 us -> 0 us
    pallas_call x1 -> x2, Pallas kernels: 84.9 us -> 77.1 us  [the longest x1 76 us: per_device(): pl.pallas_call(step_kernel, out_shape=(v((1024, 128), F32), v((256, 128),...]
    sub x2 -> x0, other arithmetic: 2.88 us -> none  [adagrad(): return (table_rows - STEP_SIZE * grad_rows / jnp.sqrt(accum_new), accum_new)]
where the time goes in v3:
time: 78 us; the launch traced here: 77.8 us
  Pallas kernels  77.1 us (99%)
    pallas_call x1, Pallas kernels, per_device(): pl.pallas_call(step_kernel, out_shape=(v((1024, 128), F32), v((256, 128),...  76 us

profile of v3, /device:TPU:1, one launch (start us, length us, event | category | flops | bytes accessed | tf_op | source)
XLA Modules:
  0.0 77.8 jit_solution(16489810219473900323)
XLA Ops:
  0.6 0.0 copy-start
  0.6 0.0 copy-start.1
  0.7 0.0 copy-start.2
  0.7 0.0 copy-start.3
  0.7 76.0 %step.1 = (f32[1024,128]{1,0:T(8,128)S(1)}, f32[256,128]{1,0:T(8,128)S(1)}) custom-call(s32[7,1024]{1,0:T(8,128)} %bitcast.4, s32[1,1,256]{2,1,0:T(1,128)} %touched_ref.1, s32[1,1,2048]{2,1,0:T(1,128)} %items_ref.1, s32[1,1,1024]{2,1,0:T(1,128)} %counts_ref.1, s32[1024,128]{1,0:T(8,128)} %bitcast.3, bf16[1024,256]{1,0:T(8,128)(2,1)} %grad_ref.1, ...), custom_call_target="tpu_custom_call" | custom-call | tf_op jit(solution)/shard_map/step/pallas_call | solution.py:317
  76.7 0.0 copy-done
  76.7 0.0 copy-done.1
  76.7 0.0 copy-done.2
  76.7 0.0 copy-done.3
  76.7 1.2 %adagrad.1 = (f32[1024,128]{1,0:T(8,128)}, f32[1024,128]{1,0:T(8,128)}, f32[256,128]{1,0:T(8,128)}, f32[256,128]{1,0:T(8,128)}) custom-call(f32[1024,128]{1,0:T(8,128)S(1)} %get-tuple-element.6.hot_grad, f32[256,128]{1,0:T(8,128)S(1)} %get-tuple-element.7.cold_grad, f32[1024,128]{1,0:T(8,128)S(1)} %copy-done, f32[1024,128]{1,0:T(8,128)S(1)} %copy-done.1, ...), custom_call_target="tpu_custom_call" | custom-call | tf_op jit(solution)/shard_map/adagrad/pallas_call | solution.py:343
Async XLA Ops:
  0.6 76.0 %copy-start = (f32[1024,128]{1,0:T(8,128)S(1)}, f32[1024,128]{1,0:T(8,128)}, u32[]{:S(2)}) copy-start(f32[1024,128]{1,0:T(8,128)} %hot.1) | copy-start | bytes 1572868
  0.6 76.0 %copy-start.1 = (f32[1024,128]{1,0:T(8,128)S(1)}, f32[1024,128]{1,0:T(8,128)}, u32[]{:S(2)}) copy-start(f32[1024,128]{1,0:T(8,128)} %hot_acc.1) | copy-start | bytes 1572868
  0.7 76.0 %copy-start.2 = (f32[256,128]{1,0:T(8,128)S(1)}, f32[256,128]{1,0:T(8,128)}, u32[]{:S(2)}) copy-start(f32[256,128]{1,0:T(8,128)} %cold.1) | copy-start | bytes 393220
  0.7 76.0 %copy-start.3 = (f32[256,128]{1,0:T(8,128)S(1)}, f32[256,128]{1,0:T(8,128)}, u32[]{:S(2)}) copy-start(f32[256,128]{1,0:T(8,128)} %cold_acc.1) | copy-start | bytes 393220

commit v4 on v3

--- a/solution.py
+++ b/solution.py
@@ -67,27 +67,22 @@
     hot_ref, cold_ref, hot_grad, cold_grad,
     full_in, full_out, full_bias, req, asked, rows_out, rows_back, member, picks, bag_mat, bag_mat_t,
     gather_t, hot_in, hot_pre, back, pooled, pool_in, bag, part, part_in, acc, acc_in, sums, outgoing,
-    arrived, hot_own, cold_own, grad_own, sem_l, sem_w, sem_pool, sem_bag, sem_a, sem_d, sem_x,
+    arrived, hot_own, cold_own, grad_own, owner_own, sem_l, sem_f, sem_w, sem_pool, sem_bag, sem_a, sem_d, sem_x,
 ):
     dp, x = lax.axis_index("dp"), lax.axis_index("mp")
     core = dp % 2
     plane = dp // 2
+    sibling = (plane * 2 + 1 - core, x)
 
     def near(ox):
         return (dp, (x + ox) % 4)
-
-    barrier = pltpu.get_barrier_semaphore()
-    for ox in range(1, 4):
-        pl.semaphore_signal(barrier, inc=1, device_id=near(ox), device_id_type=MESH)
-
-    for o in range(1, 128):
-        pl.semaphore_signal(barrier, inc=1, device_id=((dp + o) % 128, x), device_id_type=MESH)
 
     share = rows_at(x, 256)
     mine = rows_at(x, 128)
     local = [
         pltpu.make_async_copy(src, dst, sem_l.at[k])
         for k, (src, dst) in enumerate((
+            (owner_ref, owner_own),
             (cold_ref, cold_own), (win_ref, full_in.at[:, mine]), (wout_ref, full_out.at[mine]),
             (bias_ref, full_bias.at[:, mine]), (hot_ref, hot_own), (grad_ref.at[share], grad_own),
         ))
@@ -95,13 +90,21 @@
     for cp in local:
         cp.start()
 
+    barrier = pltpu.get_barrier_semaphore()
+    for ox in range(1, 4):
+        pl.semaphore_signal(barrier, inc=1, device_id=near(ox), device_id_type=MESH)
+
+    for o in range(1, 128):
+        pl.semaphore_signal(barrier, inc=1, device_id=((dp + o) % 128, x), device_id_type=MESH)
+
     touched = column(touched_ref[0].astype(F32)).astype(I32)
     lane = iota((256, 128), 1)
     owner_row = touched >> 7
     picked = jnp.concatenate(
         [ones_where(owner_row == lane + 128 * k) for k in range(8)], axis=1
     )
-    owners = owner_ref[...]
+    local[0].wait()
+    owners = owner_own[...]
     tables = jnp.concatenate(
         [(owners >> 10).astype(F32).astype(BF16), (owners & 255).astype(F32).astype(BF16)], axis=1
     )
@@ -145,13 +148,20 @@
         cp.start()
         return cp
 
+    half_in = rows_at(core, 512)
+    half_out = rows_at(core, 64)
+
+    def out_rows(index):
+        return pl.ds(pl.multiple_of(index * 128 + core * 64, 64), 64)
+
+    weight_copies = {}
+    for ox in (2, 1, 3):
+        weight_copies[ox] = (
+            to_near(ox, win_ref.at[half_in], full_in.at[half_in, mine], sem_w, ox - 1),
+            to_near(ox, wout_ref.at[half_out], full_out.at[out_rows(x)], sem_w, ox + 2),
+            to_near(ox, bias_ref, full_bias.at[:, mine], sem_w, ox + 5),
+        )
     send_all(req, asked, 0)
-
-    weight_copies = []
-    for ox in range(1, 4):
-        weight_copies.append(to_near(ox, win_ref, full_in.at[:, mine], sem_w, ox - 1))
-        weight_copies.append(to_near(ox, wout_ref, full_out.at[mine], sem_w, ox + 2))
-        weight_copies.append(to_near(ox, bias_ref, full_bias.at[:, mine], sem_w, ox + 5))
 
     counts = counts_ref[0].astype(F32)
     eight = jnp.concatenate([counts[:, 128 * j : 128 * (j + 1)] for j in range(8)], axis=0)
@@ -166,7 +176,7 @@
         start_col = column(end - eight[j : j + 1])[:, :1]
         member[128 * j : 128 * (j + 1)] = ones_where((item_pos >= start_col) & (item_pos < end_col))
     picks[...] = ones_where(items_ref[0] == iota((256, 2048), 0))
-    local[0].wait()
+    local[1].wait()
     cold_halves = halves(cold_own[...])
 
     wait_all(req, asked, 0)
@@ -179,6 +189,22 @@
     chosen = ones_where(wanted_col == (iota((512, 256), 1) + 1).astype(F32))
     rows_out[...] = joined(mm(chosen, cold_halves)).reshape(128, 4, 128)
     send_all(rows_out, rows_back, 1)
+
+    def to_sibling(ref, k):
+        cp = pltpu.make_async_remote_copy(
+            src_ref=ref, dst_ref=ref, send_sem=sem_f.at[0, k], recv_sem=sem_f.at[1, k],
+            device_id=sibling, device_id_type=MESH,
+        )
+        cp.start()
+        return cp
+
+    weight_hands = []
+    for ox in (1, 3, 2):
+        for cp in weight_copies[ox]:
+            cp.wait_recv()
+        origin = (x + 4 - ox) % 4
+        weight_hands.append(to_sibling(full_in.at[half_in, rows_at(origin, 128)], ox - 1))
+        weight_hands.append(to_sibling(full_out.at[out_rows(origin)], ox + 2))
 
     count_mat = mm_nt(member[...], picks[...]).astype(BF16)
     spot = jnp.where(bucket == iota((256, 512), 1).astype(F32), 1.0, 0.0)
@@ -186,7 +212,7 @@
     count_mat_t = mm_nt(picks[...], member[...]).astype(BF16)
     bag_mat_t[...] = mm(spot.T.astype(BF16), count_mat_t).astype(BF16)
 
-    for cp in local[1:]:
+    for cp in local[2:]:
         cp.wait()
     ids = ids_ref[:, share]
     hot_bf = hot_own[...].astype(BF16)
@@ -197,7 +223,7 @@
         gather_t[:, 256 * f : 256 * (f + 1)] = ones_where(row_of == one)
         pick_f = ones_where(column(one.astype(F32))[:, :1] == lane_1k)
         hot_in[:, 128 * f : 128 * (f + 1)] = mm(pick_f, hot_bf).astype(BF16)
-    for cp in weight_copies:
+    for cp in weight_hands:
         cp.wait_recv()
     hot_pre[...] = mm(hot_in[...], full_in[0:896]) + full_bias[...]
     back[...] = mm_nt(grad_own[...], full_out[...])
@@ -224,18 +250,20 @@
     )
 
     a_copies = []
-    for oc, ox in ((1, 2), (0, 2), (1, 1), (1, 3), (0, 1), (0, 3), (1, 0), (0, 0)):
-        there = rows_at(((core + oc) % 2) * 4 + (x + ox) % 4, 128)
-        part[there] = joined(mm(gather_t[there], in_grad))
-        k = oc * 4 + ox
-        if k:
-            cp = pltpu.make_async_remote_copy(
-                src_ref=part.at[there], dst_ref=part_in.at[k - 1], send_sem=sem_a.at[0, k - 1],
-                recv_sem=sem_a.at[1, k - 1], device_id=(plane * 2 + (core + oc) % 2, (x + ox) % 4),
-                device_id_type=MESH,
-            )
-            cp.start()
-            a_copies.append(cp)
+    for oc in (1, 0):
+        side = (core + oc) % 2
+        half = rows_at(side, 512)
+        part[half] = joined(mm(gather_t[half], in_grad))
+        for ox in (2, 1, 3, 0):
+            k = oc * 4 + ox
+            if k:
+                cp = pltpu.make_async_remote_copy(
+                    src_ref=part.at[rows_at(side * 4 + (x + ox) % 4, 128)], dst_ref=part_in.at[k - 1],
+                    send_sem=sem_a.at[0, k - 1], recv_sem=sem_a.at[1, k - 1],
+                    device_id=(plane * 2 + side, (x + ox) % 4), device_id_type=MESH,
+                )
+                cp.start()
+                a_copies.append(cp)
     bag_copies = [to_near(ox, bag.at[x], bag.at[x], sem_bag, ox - 1) for ox in (2, 1, 3)]
     for cp in a_copies:
         cp.wait_recv()
@@ -286,7 +314,6 @@
         cp.start()
         return cp
 
-    sibling = (plane * 2 + 1 - core, x)
     d_copies = [spread_block(own, near(ox), ox - 1) for ox in (1, 2, 3)]
     forwards = [spread_block(own, sibling, 3)]
     for ox in (1, 3, 2):
@@ -298,7 +325,7 @@
     for cp in forwards:
         cp.wait_recv()
 
-    for cp in weight_copies + pool_copies + bag_copies + a_copies + d_copies + forwards:
+    for cp in [c for cs in weight_copies.values() for c in cs] + weight_hands + pool_copies + bag_copies + a_copies + d_copies + forwards:
         cp.wait_send()
     wait_sent(req, 0)
     wait_sent(rows_out, 1)
@@ -317,7 +344,7 @@
     hot_grad, cold_grad = pl.pallas_call(
         step_kernel,
         out_shape=(v((1024, 128), F32), v((256, 128), F32)),
-        in_specs=[vmem] * 5 + [pl.BlockSpec(memory_space=pl.ANY)] * 6,
+        in_specs=[vmem] * 4 + [pl.BlockSpec(memory_space=pl.ANY)] * 7,
         out_specs=(vmem, vmem),
         scratch_shapes=[
             v((1024, 512), BF16), v((512, 256), BF16), v((1, 512), F32),
@@ -329,7 +356,7 @@
             v((1024, 128), F32), v((7, 128, 128), F32), v((64, 2, 128), F32), v((64, 2, 128), F32),
             v((64, 2, 128), F32),
             v((128, 4, 128), F32), v((128, 4, 128), F32),
-            v((1024, 128), F32), v((256, 128), F32), v((256, 256), BF16), dma((6,)),
+            v((1024, 128), F32), v((256, 128), F32), v((256, 256), BF16), v((1024, 128), I32), dma((7,)), dma((2, 6)),
             dma((2, 9)), dma((2, 3)), dma((2, 3)), dma((2, 7)), dma((2, 7)), dma((2, 5)),
         ],
         compiler_params=pltpu.CompilerParams(

time: 78 us -> 79.6 us (1.021)
  Pallas kernels: 77.1 us -> 78.7 us
    pallas_call x1, Pallas kernels: 76 us -> 77.6 us  [per_device(): pl.pallas_call(step_kernel, out_shape=(v((1024, 128), F32), v((256, 128),...]
where the time goes in v4:
time: 79.6 us; the launch traced here: 79.4 us
  Pallas kernels  78.7 us (99%)
    pallas_call x1, Pallas kernels, per_device(): pl.pallas_call(step_kernel, out_shape=(v((1024, 128), F32), v((256, 128),...  77.6 us

profile of v4, /device:TPU:1, one launch (start us, length us, event | category | flops | bytes accessed | tf_op | source)
XLA Modules:
  0.0 79.4 jit_solution(1595340329865121512)
XLA Ops:
  0.6 0.0 copy-start
  0.6 0.0 copy-start.1
  0.7 0.0 copy-start.2
  0.7 0.0 copy-start.3
  0.7 77.6 %step.1 = (f32[1024,128]{1,0:T(8,128)S(1)}, f32[256,128]{1,0:T(8,128)S(1)}) custom-call(s32[7,1024]{1,0:T(8,128)} %bitcast.4, s32[1,1,256]{2,1,0:T(1,128)} %touched_ref.1, s32[1,1,2048]{2,1,0:T(1,128)} %items_ref.1, s32[1,1,1024]{2,1,0:T(1,128)} %counts_ref.1, s32[1024,128]{1,0:T(8,128)} %bitcast.3, bf16[1024,256]{1,0:T(8,128)(2,1)} %grad_ref.1, ...), custom_call_target="tpu_custom_call" | custom-call | tf_op jit(solution)/shard_map/step/pallas_call | solution.py:344
  78.2 0.0 copy-done
  78.2 0.0 copy-done.1
  78.3 0.0 copy-done.2
  78.3 0.0 copy-done.3
  78.3 1.2 %adagrad.1 = (f32[1024,128]{1,0:T(8,128)}, f32[1024,128]{1,0:T(8,128)}, f32[256,128]{1,0:T(8,128)}, f32[256,128]{1,0:T(8,128)}) custom-call(f32[1024,128]{1,0:T(8,128)S(1)} %get-tuple-element.6.hot_grad, f32[256,128]{1,0:T(8,128)S(1)} %get-tuple-element.7.cold_grad, f32[1024,128]{1,0:T(8,128)S(1)} %copy-done, f32[1024,128]{1,0:T(8,128)S(1)} %copy-done.1, ...), custom_call_target="tpu_custom_call" | custom-call | tf_op jit(solution)/shard_map/adagrad/pallas_call | solution.py:370
Async XLA Ops:
  0.6 77.6 %copy-start = (f32[1024,128]{1,0:T(8,128)S(1)}, f32[1024,128]{1,0:T(8,128)}, u32[]{:S(2)}) copy-start(f32[1024,128]{1,0:T(8,128)} %hot.1) | copy-start | bytes 1572868
  0.6 77.6 %copy-start.1 = (f32[1024,128]{1,0:T(8,128)S(1)}, f32[1024,128]{1,0:T(8,128)}, u32[]{:S(2)}) copy-start(f32[1024,128]{1,0:T(8,128)} %hot_acc.1) | copy-start | bytes 1572868
  0.7 77.6 %copy-start.2 = (f32[256,128]{1,0:T(8,128)S(1)}, f32[256,128]{1,0:T(8,128)}, u32[]{:S(2)}) copy-start(f32[256,128]{1,0:T(8,128)} %cold.1) | copy-start | bytes 393220
  0.7 77.6 %copy-start.3 = (f32[256,128]{1,0:T(8,128)S(1)}, f32[256,128]{1,0:T(8,128)}, u32[]{:S(2)}) copy-start(f32[256,128]{1,0:T(8,128)} %cold_acc.1) | copy-start | bytes 393220

commit v5 on v3

--- a/solution.py
+++ b/solution.py
@@ -120,8 +120,7 @@
     pl.semaphore_wait(barrier, 130)
 
     def send_all(src, dst, k):
-        @pl.loop(1, 128)
-        def _(o):
+        for o in range(1, 128):
             to = (dp + o) % 128
             pltpu.make_async_remote_copy(
                 src_ref=src.at[to], dst_ref=dst.at[dp], send_sem=sem_x.at[0, k], recv_sem=sem_x.at[1, k],
@@ -244,8 +243,7 @@
         block = block + part_in[k]
     acc[...] = block.reshape(64, 2, 128)
 
-    @pl.loop(1, 64)
-    def _(o):
+    for o in range(1, 64):
         to = (plane + o) % 64
         pltpu.make_async_remote_copy(
             src_ref=acc.at[to], dst_ref=acc_in.at[plane], send_sem=sem_x.at[0, 2], recv_sem=sem_x.at[1, 2],
@@ -257,8 +255,7 @@
     pltpu.make_async_copy(acc_in.at[pl.ds(0, 63)], acc_in.at[pl.ds(0, 63)], sem_x.at[1, 2]).wait()
     sums[plane] = jnp.sum(acc_in[...], axis=0)
 
-    @pl.loop(1, 64)
-    def _(o):
+    for o in range(1, 64):
         to = (plane + o) % 64
         pltpu.make_async_remote_copy(
             src_ref=sums.at[plane], dst_ref=sums.at[plane], send_sem=sem_x.at[0, 3], recv_sem=sem_x.at[1, 3],

time: 78 us -> 78.5 us (level)
  no operation moved by 1% of the time
where the time goes in v5:
time: 78.5 us; the launch traced here: 78.4 us
  Pallas kernels  77.7 us (99%)
    pallas_call x1, Pallas kernels, per_device(): pl.pallas_call(step_kernel, out_shape=(v((1024, 128), F32), v((256, 128),...  76.5 us

profile of v5, /device:TPU:1, one launch (start us, length us, event | category | flops | bytes accessed | tf_op | source)
XLA Modules:
  0.0 78.4 jit_solution(4715736389638460378)
XLA Ops:
  0.6 0.0 copy-start
  0.6 0.0 copy-start.1
  0.7 0.0 copy-start.2
  0.7 0.0 copy-start.3
  0.7 76.5 %step.1 = (f32[1024,128]{1,0:T(8,128)S(1)}, f32[256,128]{1,0:T(8,128)S(1)}) custom-call(s32[7,1024]{1,0:T(8,128)} %bitcast.4, s32[1,1,256]{2,1,0:T(1,128)} %touched_ref.1, s32[1,1,2048]{2,1,0:T(1,128)} %items_ref.1, s32[1,1,1024]{2,1,0:T(1,128)} %counts_ref.1, s32[1024,128]{1,0:T(8,128)} %bitcast.3, bf16[1024,256]{1,0:T(8,128)(2,1)} %grad_ref.1, ...), custom_call_target="tpu_custom_call" | custom-call | tf_op jit(solution)/shard_map/step/pallas_call | solution.py:314
  77.2 0.0 copy-done
  77.2 0.0 copy-done.1
  77.2 0.0 copy-done.2
  77.2 0.0 copy-done.3
  77.2 1.2 %adagrad.1 = (f32[1024,128]{1,0:T(8,128)}, f32[1024,128]{1,0:T(8,128)}, f32[256,128]{1,0:T(8,128)}, f32[256,128]{1,0:T(8,128)}) custom-call(f32[1024,128]{1,0:T(8,128)S(1)} %get-tuple-element.6.hot_grad, f32[256,128]{1,0:T(8,128)S(1)} %get-tuple-element.7.cold_grad, f32[1024,128]{1,0:T(8,128)S(1)} %copy-done, f32[1024,128]{1,0:T(8,128)S(1)} %copy-done.1, ...), custom_call_target="tpu_custom_call" | custom-call | tf_op jit(solution)/shard_map/adagrad/pallas_call | solution.py:340
Async XLA Ops:
  0.6 76.6 %copy-start = (f32[1024,128]{1,0:T(8,128)S(1)}, f32[1024,128]{1,0:T(8,128)}, u32[]{:S(2)}) copy-start(f32[1024,128]{1,0:T(8,128)} %hot.1) | copy-start | bytes 1572868
  0.6 76.6 %copy-start.1 = (f32[1024,128]{1,0:T(8,128)S(1)}, f32[1024,128]{1,0:T(8,128)}, u32[]{:S(2)}) copy-start(f32[1024,128]{1,0:T(8,128)} %hot_acc.1) | copy-start | bytes 1572868
  0.7 76.6 %copy-start.2 = (f32[256,128]{1,0:T(8,128)S(1)}, f32[256,128]{1,0:T(8,128)}, u32[]{:S(2)}) copy-start(f32[256,128]{1,0:T(8,128)} %cold.1) | copy-start | bytes 393220
  0.7 76.6 %copy-start.3 = (f32[256,128]{1,0:T(8,128)S(1)}, f32[256,128]{1,0:T(8,128)}, u32[]{:S(2)}) copy-start(f32[256,128]{1,0:T(8,128)} %cold_acc.1) | copy-start | bytes 393220

commit v6 on v3

--- a/solution.py
+++ b/solution.py
@@ -254,6 +254,11 @@
 
     acc_in[plane] = acc[plane]
 
+    for cp in bag_copies:
+        cp.wait_recv()
+    bag_all = halves(bag[...].reshape(1024, 128))
+    outgoing[...] = joined(mm(bag_mat_t[...], bag_all)).reshape(128, 4, 128)
+
     pltpu.make_async_copy(acc_in.at[pl.ds(0, 63)], acc_in.at[pl.ds(0, 63)], sem_x.at[1, 2]).wait()
     sums[plane] = jnp.sum(acc_in[...], axis=0)
 
@@ -264,11 +269,6 @@
             src_ref=sums.at[plane], dst_ref=sums.at[plane], send_sem=sem_x.at[0, 3], recv_sem=sem_x.at[1, 3],
             device_id=(to * 2 + core, x), device_id_type=MESH,
         ).start()
-
-    for cp in bag_copies:
-        cp.wait_recv()
-    bag_all = halves(bag[...].reshape(1024, 128))
-    outgoing[...] = joined(mm(bag_mat_t[...], bag_all)).reshape(128, 4, 128)
 
     send_all(outgoing, arrived, 4)
     wanted_rows = jnp.broadcast_to(wanted_col, (512, 128)).T[0:1]

time: 78 us -> 78 us (level)
  no operation moved by 1% of the time
where the time goes in v6:
time: 78 us; the launch traced here: 77.8 us
  Pallas kernels  77.1 us (99%)
    pallas_call x1, Pallas kernels, per_device(): pl.pallas_call(step_kernel, out_shape=(v((1024, 128), F32), v((256, 128),...  76 us

profile of v6, /device:TPU:1, one launch (start us, length us, event | category | flops | bytes accessed | tf_op | source)
XLA Modules:
  0.0 77.8 jit_solution(5518067505308351050)
XLA Ops:
  0.6 0.0 copy-start
  0.6 0.0 copy-start.1
  0.7 0.0 copy-start.2
  0.7 0.0 copy-start.3
  0.7 76.0 %step.1 = (f32[1024,128]{1,0:T(8,128)S(1)}, f32[256,128]{1,0:T(8,128)S(1)}) custom-call(s32[7,1024]{1,0:T(8,128)} %bitcast.4, s32[1,1,256]{2,1,0:T(1,128)} %touched_ref.1, s32[1,1,2048]{2,1,0:T(1,128)} %items_ref.1, s32[1,1,1024]{2,1,0:T(1,128)} %counts_ref.1, s32[1024,128]{1,0:T(8,128)} %bitcast.3, bf16[1024,256]{1,0:T(8,128)(2,1)} %grad_ref.1, ...), custom_call_target="tpu_custom_call" | custom-call | tf_op jit(solution)/shard_map/step/pallas_call | solution.py:317
  76.6 0.0 copy-done
  76.6 0.0 copy-done.1
  76.7 0.0 copy-done.2
  76.7 0.0 copy-done.3
  76.7 1.2 %adagrad.1 = (f32[1024,128]{1,0:T(8,128)}, f32[1024,128]{1,0:T(8,128)}, f32[256,128]{1,0:T(8,128)}, f32[256,128]{1,0:T(8,128)}) custom-call(f32[1024,128]{1,0:T(8,128)S(1)} %get-tuple-element.6.hot_grad, f32[256,128]{1,0:T(8,128)S(1)} %get-tuple-element.7.cold_grad, f32[1024,128]{1,0:T(8,128)S(1)} %copy-done, f32[1024,128]{1,0:T(8,128)S(1)} %copy-done.1, ...), custom_call_target="tpu_custom_call" | custom-call | tf_op jit(solution)/shard_map/adagrad/pallas_call | solution.py:343
Async XLA Ops:
  0.6 76.0 %copy-start = (f32[1024,128]{1,0:T(8,128)S(1)}, f32[1024,128]{1,0:T(8,128)}, u32[]{:S(2)}) copy-start(f32[1024,128]{1,0:T(8,128)} %hot.1) | copy-start | bytes 1572868
  0.6 76.0 %copy-start.1 = (f32[1024,128]{1,0:T(8,128)S(1)}, f32[1024,128]{1,0:T(8,128)}, u32[]{:S(2)}) copy-start(f32[1024,128]{1,0:T(8,128)} %hot_acc.1) | copy-start | bytes 1572868
  0.7 76.0 %copy-start.2 = (f32[256,128]{1,0:T(8,128)S(1)}, f32[256,128]{1,0:T(8,128)}, u32[]{:S(2)}) copy-start(f32[256,128]{1,0:T(8,128)} %cold.1) | copy-start | bytes 393220
  0.7 76.0 %copy-start.3 = (f32[256,128]{1,0:T(8,128)S(1)}, f32[256,128]{1,0:T(8,128)}, u32[]{:S(2)}) copy-start(f32[256,128]{1,0:T(8,128)} %cold_acc.1) | copy-start | bytes 393220
